TPU v7x, 768 devices: a whole 4x8x12 slice. The times are simulated.
768 devices in a mesh: segment: 16 (over y, core), dp: 3 (over z_hi), expert: 16 (over x, z_lo).
Axes of the slice: x: 4, y: 8, z: 12 (z_hi: 3, z_lo: 4; z = z_hi * 4 + z_lo), core: 2. Of those that a mesh axis runs over, the one named last changes fastest.
Arguments:
- saved_b: bfloat16 [16, 6144, 2048], P('segment', ('dp', 'expert')), may hold values from -6 to 6
- route_b: int32 [16, 6144, 1], P('segment', ('dp', 'expert')), may hold values from 0 to 15; in each aligned block of 128 rows (0 to 127, 128 to 255, ..., all dimensions but the last counted through in order) at most 10 rows name the same one
- gate_b: float32 [16, 6144, 1], P('segment', ('dp', 'expert')), may hold values from 0.2 to 1
- grad_y_b: bfloat16 [16, 6144, 2048], P('segment', ('dp', 'expert')), may hold values from -6 to 6
- w_in: bfloat16 [16, 16, 2048, 768], P('segment', 'expert'), may hold values from -0.125 to 0.125
- w_out: bfloat16 [16, 16, 768, 2048], P('segment', 'expert'), may hold values from -0.21875 to 0.21875
Outputs:
- grad_x_b: bfloat16 [16, 6144, 2048], P('segment', ('dp', 'expert'))
- grad_in: bfloat16 [16, 16, 2048, 768], P('segment', 'expert', None, 'dp')
Inputs may be any that keep to these rules, and one draw needn't show every extreme that they name: `route_b`: of the 128 tokens of one device of a section, at most 10 pick any one expert; some device sends exactly 10 to some expert.
All inputs are finite; a program needn't handle non-finite values.
Results may differ from a plain program's by a relative error of at most 0.01.
Values may be sent and summed in bfloat16 or wider, within the bound.
No kernel may reach another device: no remote copies, remote signals or barrier semaphores. Data moves between devices by JAX's collectives and lax.ppermute only.
A program may use at most 64 MiB of HBM per device.

v0:
```python
import jax
import jax.numpy as jnp
from jax import lax
from jax.sharding import PartitionSpec as P


def passed_along(value, axis, steps):
    count = lax.axis_size(axis)
    pairs = [(source, (source + steps) % count) for source in range(count)]
    return lax.ppermute(value, axis, pairs)


def silu_grad(value):
    sigma = jax.nn.sigmoid(value)
    return sigma * (1.0 + value * (1.0 - sigma))


def slot_table(expert_ids, capacity, experts):
    onehot = (expert_ids[:, None] == jnp.arange(experts, dtype=jnp.int32)[None, :]).astype(
        jnp.int32
    )
    before = jnp.cumsum(onehot, axis=0) - onehot
    position = expert_ids * capacity + jnp.sum(before * onehot, axis=1)
    slot_ids = jnp.arange(experts * capacity, dtype=jnp.int32)
    return (slot_ids[:, None] == position[None, :]).astype(jnp.bfloat16)


def dispatch(table, values, experts, capacity):
    placed = jnp.dot(table, values, preferred_element_type=jnp.float32).astype(jnp.bfloat16)
    return placed.reshape(experts, capacity, values.shape[1])


def combine(table, rows):
    return lax.dot_general(
        table, rows, (((0,), (0,)), ((), ())), preferred_element_type=jnp.float32
    )


def body(saved_b, route_b, gate_b, grad_y_b, w_in, w_out):
    experts = lax.axis_size("expert")
    tok_rows = saved_b.shape[1]
    model_width = saved_b.shape[2]
    capacity = max(2, tok_rows * 5 // (4 * experts))
    arrived = passed_along(grad_y_b, "segment", -1)[0]
    table_b = slot_table(route_b[0, :, 0], capacity, experts)
    scaled = (gate_b[0] * arrived.astype(jnp.float32)).astype(jnp.bfloat16)
    send_x = dispatch(table_b, saved_b[0], experts, capacity)
    send_g = dispatch(table_b, scaled, experts, capacity)
    recv_x, recv_g = (
        lax.all_to_all(send_x, "expert", split_axis=0, concat_axis=0, tiled=True),
        lax.all_to_all(send_g, "expert", split_axis=0, concat_axis=0, tiled=True),
    )
    rows_x = recv_x.reshape(-1, model_width)
    rows_g = recv_g.reshape(-1, model_width)
    weight_in = w_in[0, 0]
    weight_out = w_out[0, 0]
    pre_b = jnp.dot(rows_x, weight_in, preferred_element_type=jnp.float32)
    grad_h = lax.dot_general(
        rows_g, weight_out, (((1,), (1,)), ((), ())), preferred_element_type=jnp.float32
    )
    grad_pre = (grad_h * silu_grad(pre_b)).astype(jnp.bfloat16)
    grad_rows_x = lax.dot_general(
        grad_pre, weight_in, (((1,), (1,)), ((), ())), preferred_element_type=jnp.float32
    ).astype(jnp.bfloat16)
    back_x = lax.all_to_all(
        grad_rows_x.reshape(experts, capacity, model_width),
        "expert",
        split_axis=0,
        concat_axis=0,
        tiled=True,
    )
    grad_x = combine(table_b, back_x.reshape(-1, model_width)).astype(jnp.bfloat16)
    term_in = lax.dot_general(
        rows_x, grad_pre, (((0,), (0,)), ((), ())), preferred_element_type=jnp.float32
    )
    summed_in = lax.psum_scatter(
        term_in.astype(jnp.bfloat16), "dp", scatter_dimension=1, tiled=True
    )
    return (grad_x[None], summed_in[None, None])


def solution(mesh):
    return jax.shard_map(
        body,
        mesh=mesh,
        in_specs=(
            P("segment", ("dp", "expert"), None),
            P("segment", ("dp", "expert"), None),
            P("segment", ("dp", "expert"), None),
            P("segment", ("dp", "expert"), None),
            P("segment", "expert", None, None),
            P("segment", "expert", None, None),
        ),
        out_specs=(P("segment", ("dp", "expert"), None), P("segment", "expert", None, "dp")),
        check_vma=False,
    )
```

profile of v0, /device:TPU:79, one launch (start us, length us, event | category | flops | bytes accessed | tf_op | source)
XLA Modules:
  0.0 230.2 jit_solution(15046595966785423512)
XLA Ops:
  7.2 0.0 copy-start
  7.2 0.0 copy-start.2
  7.2 0.9 fusion.21
  8.1 0.2 reduce_window_sum.11
  8.3 0.8 select_reduce_fusion
  9.1 0.7 multiply_add_fusion
  9.8 2.2 convolution_convert_fusion.1
  12.0 2.2 reshape.36
  14.2 8.8 %all-to-all-start.1 = ((bf16[16,10,2048]{2,1,0:T(8,128)(2,1)}), bf16[16,10,2048]{2,1,0:T(8,128)(2,1)}, u32[]{:S(2)}, u32[]{:S(2)}) async-start(bf16[16,10,2048]{2,1,0:T(8,128)(2,1)} %reshape.36), calls=%async_computation.1 | async-start | bytes 2097152 | tf_op jit(solution)/shard_map/all_to_all | solution.py:50
  22.9 1.2 collective-permute-start
  24.2 8.3 %collective-permute-done = bf16[1,128,2048]{2,1,0:T(8,128)(2,1)S(1)} collective-permute-done((bf16[1,128,2048]{2,1,0:T(8,128)(2,1)}, bf16[1,128,2048]{2,1,0:T(8,128)(2,1)S(1)}, u32[]{:S(2)}, u32[]{:S(2)}) %collective-permute-start) | collective-permute-done | bytes 524320 | tf_op jit(solution)/shard_map/ppermute | solution.py:10
  32.4 0.0 copy-done.2
  32.4 1.3 convolution_convert_fusion.2
  33.7 2.2 reshape.34
  35.8 10.3 %all-to-all-done.1 = bf16[16,10,2048]{2,1,0:T(8,128)(2,1)} async-done(((bf16[16,10,2048]{2,1,0:T(8,128)(2,1)}), bf16[16,10,2048]{2,1,0:T(8,128)(2,1)}, u32[]{:S(2)}, u32[]{:S(2)}) %all-to-all-start.1) | async-done | bytes 655392 | tf_op jit(solution)/shard_map/all_to_all | solution.py:50
  46.2 8.3 %all-to-all-start = ((bf16[16,10,2048]{2,1,0:T(8,128)(2,1)}), bf16[16,10,2048]{2,1,0:T(8,128)(2,1)}, u32[]{:S(2)}, u32[]{:S(2)}) async-start(bf16[16,10,2048]{2,1,0:T(8,128)(2,1)} %reshape.34), calls=%async_computation | async-start | bytes 2097152 | tf_op jit(solution)/shard_map/all_to_all | solution.py:51
  54.4 0.0 reduce-scatter.2.cloned.1.call-start
  54.5 2.2 reshape.37
  56.7 0.0 copy-done
  56.7 2.5 %fusion.2 = f32[160,768]{1,0:T(8,128)} fusion(bf16[160,2048]{1,0:T(8,128)(2,1)} %reshape.37, bf16[1,1,2048,768]{3,2,1,0:T(8,128)(2,1)S(1)} %copy-done), kind=kOutput, calls=%fused_computation.3 | convolution fusion | flops 503316480 | bytes 4292608 | tf_op jit(solution)/shard_map/dot_general | solution.py:57
  59.2 18.4 %all-to-all-done = bf16[16,10,2048]{2,1,0:T(8,128)(2,1)} async-done(((bf16[16,10,2048]{2,1,0:T(8,128)(2,1)}), bf16[16,10,2048]{2,1,0:T(8,128)(2,1)}, u32[]{:S(2)}, u32[]{:S(2)}) %all-to-all-start) | async-done | bytes 655392 | tf_op jit(solution)/shard_map/all_to_all | solution.py:51
  77.6 2.1 reshape.35
  79.8 3.4 %fusion.13 = bf16[160,768]{1,0:T(8,128)(2,1)S(1)} fusion(bf16[160,2048]{1,0:T(8,128)(2,1)} %reshape.35, bf16[1,1,768,2048]{3,2,1,0:T(8,128)(2,1)} %param.11, f32[160,768]{1,0:T(8,128)} %fusion.2), kind=kOutput, calls=%fused_computation.13 | convolution fusion | flops 504422400 | bytes 4538368 | tf_op jit(solution)/shard_map/dot_general | solution.py:58
  83.2 0.0 copy-done.1
  83.2 2.7 %convolution_convert_fusion = bf16[2048,768]{1,0:T(8,128)(2,1)} fusion(bf16[160,2048]{1,0:T(8,128)(2,1)S(1)} %copy-done.1, bf16[160,768]{1,0:T(8,128)(2,1)S(1)} %fusion.13), kind=kOutput, calls=%fused_computation | convolution fusion | flops 504889344 | bytes 4046848 | tf_op jit(solution)/shard_map/dot_general | solution.py:73
  85.9 0.0 reduce-scatter.2.cloned.1.call-update
  86.0 2.0 fusion.6
  88.0 2.2 reshape.38
  90.1 96.4 %all_to_all.15 = bf16[16,10,2048]{2,1,0:T(8,128)(2,1)} all-to-all(bf16[16,10,2048]{2,1,0:T(8,128)(2,1)} %reshape.38), channel_id=1, replica_groups=mesh['segment'=16,'dp'=3,'expert'=16] {'expert'}, dimensions={0} | all-to-all | bytes 1310720 | tf_op jit(solution)/shard_map/all_to_all | solution.py:65
  186.5 2.2 reshape.39
  188.7 2.2 fusion.9
  190.9 32.4 %reduce-scatter.2.cloned.1.call-done = bf16[2048,256]{1,0:T(8,128)(2,1)} async-done(((bf16[2048,768]{1,0:T(8,128)(2,1)}), bf16[2048,256]{1,0:T(8,128)(2,1)}) %reduce-scatter.2.cloned.1.call-update) | async-done | bytes 1048592 | tf_op jit(solution)/shard_map/reduce_scatter | solution.py:76
  (1 shorter events, 0.0 us)
Async XLA Ops:
  7.2 49.5 %copy-start = (bf16[1,1,2048,768]{3,2,1,0:T(8,128)(2,1)S(1)}, bf16[1,1,2048,768]{3,2,1,0:T(8,128)(2,1)}, u32[]{:S(2)}) copy-start(bf16[1,1,2048,768]{3,2,1,0:T(8,128)(2,1)} %param.10) | copy-start | bytes 9437188
  7.2 25.2 %copy-start.2 = (f32[1,128,1]{1,2,0:T(1,128)S(1)}, f32[1,128,1]{1,2,0:T(1,128)}, u32[]{:S(2)}) copy-start(f32[1,128,1]{1,2,0:T(1,128)} %param.8) | copy-start | bytes 1540
  14.2 32.0 %all-to-all-start.1 = ((bf16[16,10,2048]{2,1,0:T(8,128)(2,1)}), bf16[16,10,2048]{2,1,0:T(8,128)(2,1)}, u32[]{:S(2)}, u32[]{:S(2)}) async-start(bf16[16,10,2048]{2,1,0:T(8,128)(2,1)} %reshape.36), calls=%async_computation.1 | async-start | bytes 2097152 | tf_op jit(solution)/shard_map/all_to_all | solution.py:50
  22.9 9.5 %collective-permute-start = (bf16[1,128,2048]{2,1,0:T(8,128)(2,1)}, bf16[1,128,2048]{2,1,0:T(8,128)(2,1)S(1)}, u32[]{:S(2)}, u32[]{:S(2)}) collective-permute-start(bf16[1,128,2048]{2,1,0:T(8,128)(2,1)} %param.9), channel_id=1, source_target_pairs={{0,720},{48,0},{96,48},{144,96},{192,144},{240,192},{288,240},{336... | collective-permute-start | bytes 1572872 | tf_op jit(solution)/shard_map/ppermute | solution.py:10
  46.2 31.5 %all-to-all-start = ((bf16[16,10,2048]{2,1,0:T(8,128)(2,1)}), bf16[16,10,2048]{2,1,0:T(8,128)(2,1)}, u32[]{:S(2)}, u32[]{:S(2)}) async-start(bf16[16,10,2048]{2,1,0:T(8,128)(2,1)} %reshape.34), calls=%async_computation | async-start | bytes 2097152 | tf_op jit(solution)/shard_map/all_to_all | solution.py:51
  54.4 168.9 %reduce-scatter.2.cloned.1.call-start = ((), (), s32[]{:S(2)}) async-start(), calls=%async_computation.4 | async-start | bytes 4194304 | tf_op jit(solution)/shard_map/reduce_scatter | solution.py:76
  79.8 3.4 %copy-start.1 = (bf16[160,2048]{1,0:T(8,128)(2,1)S(1)}, bf16[160,2048]{1,0:T(8,128)(2,1)}, u32[]{:S(2)}) copy-start(bf16[160,2048]{1,0:T(8,128)(2,1)} %reshape.37) | copy-start | bytes 1966084
Sparse Core Ops, SparseCore 0:
  86.1 137.1 reduce-scatter.1
where the time goes:
time: 231 us; the launch traced here: 230 us
  blocking collectives  96.4 us (42%)
  waiting for transfers between devices  69.4 us (30%)
  starting transfers between devices  18.3 us (8%)
  matrix products  16.4 us (7%)
  between operations  14.1 us (6%)
  local copies, waits for them, and re-layouts  13 us (6%)
  other arithmetic  2.56 us (1%)
    all_to_all x1, blocking collectives, body(): lax.all_to_all(grad_rows_x.reshape(experts, capacity, model_width), 'expe...  96.4 us
    reduce_scatter x1, waiting for transfers between devices, body(): lax.psum_scatter(term_in.astype(jnp.bfloat16), 'dp', scatter_dimension=1,...  32.4 us
    all_to_all x1, waiting for transfers between devices, body(): lax.all_to_all(send_g, 'expert', split_axis=0, concat_axis=0, tiled=True)  18.4 us
    all_to_all x1, waiting for transfers between devices, body(): lax.all_to_all(send_x, 'expert', split_axis=0, concat_axis=0, tiled=True)  10.3 us
    all_to_all x1, starting transfers between devices, body(): lax.all_to_all(send_x, 'expert', split_axis=0, concat_axis=0, tiled=True)  8.75 us
    all_to_all x1, starting transfers between devices, body(): lax.all_to_all(send_g, 'expert', split_axis=0, concat_axis=0, tiled=True)  8.28 us
    ppermute x1, waiting for transfers between devices, passed_along(): return lax.ppermute(value, axis, pairs)  8.26 us
  transfers between devices with their start and end apart: 4, of which 4 were waited for; matrix products, arithmetic and copies ran while one was open for 7% of the time, Pallas kernels for 0%

commit v1 on v0

v1 whole, which is shorter than its diff:
```python
import functools

import jax
import jax.numpy as jnp
from jax import lax
from jax.experimental import pallas as pl
from jax.experimental.pallas import tpu as pltpu
from jax.sharding import PartitionSpec as P

PIECES = 4
F32 = jnp.float32
BF16 = jnp.bfloat16


def passed_along(value, axis, steps):
    count = lax.axis_size(axis)
    pairs = [(source, (source + steps) % count) for source in range(count)]
    return lax.ppermute(value, axis, pairs)


def silu_grad(value):
    sigma = jax.nn.sigmoid(value)
    return sigma * (1.0 + value * (1.0 - sigma))


def iota(shape, dim):
    return lax.broadcasted_iota(jnp.int32, shape, dim)


def one_hot(condition):
    return jnp.where(condition, 1.0, 0.0).astype(BF16)


def dot(a, b, contract=((1,), (0,))):
    return lax.dot_general(a, b, (contract, ((), ())), preferred_element_type=F32)


def slots_along_lanes(route, experts, capacity):
    tokens = route.shape[0]
    square = (tokens, tokens)
    lane_route = jnp.sum(
        jnp.where(iota(square, 0) == iota(square, 1), route.astype(F32), 0.0), axis=0, keepdims=True
    )
    named = one_hot(iota((experts, tokens), 0).astype(F32) == lane_route)
    before = dot(named, one_hot(iota(square, 0) < iota(square, 1)))
    rank = jnp.sum(before * named.astype(F32), axis=0, keepdims=True)
    return (lane_route * (PIECES * capacity) + rank).astype(jnp.int32)


def slots_along_sublanes(route, capacity):
    tokens = route.shape[0]
    square = (tokens, tokens)
    named = one_hot(iota(square, 1) == route)
    before = dot(one_hot(iota(square, 1) < iota(square, 0)), named)
    rank = jnp.sum(before * named.astype(F32), axis=1, keepdims=True)
    return route * (PIECES * capacity) + rank.astype(jnp.int32)


def place(slot, values, capacity, rows):
    tokens, width = values.shape
    short = width // PIECES
    at = iota((rows, tokens), 0)
    table = jnp.concatenate([one_hot(at == slot + p * capacity) for p in range(PIECES)], axis=1)
    stacked = jnp.concatenate([values[:, p * short : (p + 1) * short] for p in range(PIECES)], axis=0)
    return dot(table, stacked).astype(BF16)


def dispatch_x_kernel(capacity, experts, route_ref, values_ref, out_ref):
    slot = slots_along_lanes(route_ref[...], experts, capacity)
    out_ref[...] = place(slot, values_ref[...], capacity, out_ref.shape[0])


def dispatch_g_kernel(capacity, experts, route_ref, gate_ref, values_ref, out_ref):
    slot = slots_along_lanes(route_ref[...], experts, capacity)
    scaled = (gate_ref[...] * values_ref[...].astype(F32)).astype(BF16)
    out_ref[...] = place(slot, scaled, capacity, out_ref.shape[0])


def combine_kernel(capacity, route_ref, rows_ref, out_ref):
    slot = slots_along_sublanes(route_ref[...], capacity)
    rows = rows_ref[...]
    count, short = rows.shape
    at = iota((slot.shape[0], count), 1)
    for p in range(PIECES):
        table = one_hot(at == slot + p * capacity)
        out_ref[:, p * short : (p + 1) * short] = dot(table, rows).astype(BF16)


def short_row(capacity, row, piece):
    group = (row * (65536 // capacity + 1)) >> 16
    return row + group * ((PIECES - 1) * capacity) + piece * capacity


def whole_piece(capacity, rows, piece):
    count = rows.shape[0]
    shape = (count // PIECES, count)
    pick = one_hot(iota(shape, 1) == short_row(capacity, iota(shape, 0), piece))
    return dot(pick, rows).astype(BF16)


def pre_kernel(capacity, rows_ref, w_in_ref, pre_ref):
    rows = rows_ref[...]
    short = rows.shape[1]
    total = None
    for p in range(PIECES):
        term = dot(whole_piece(capacity, rows, p), w_in_ref[p * short : (p + 1) * short, :])
        total = term if total is None else total + term
    pre_ref[...] = total


def expert_kernel(capacity, parts, place_ref, rows_ref, pre_ref, w_in_ref, w_out_ref,
                  back_ref, own_ref, up_ref, down_ref, hold_ref):
    rows = rows_ref[...]
    count, short = rows.shape
    total = None
    for p in range(PIECES):
        term = dot(whole_piece(capacity, rows, p), w_out_ref[:, p * short : (p + 1) * short], ((1,), (1,)))
        total = term if total is None else total + term
    grad_pre = (total * silu_grad(pre_ref[...])).astype(BF16)
    hold_ref[...] = grad_pre
    shape = (count, count // PIECES)
    back = None
    for p in range(PIECES):
        piece = dot(grad_pre, w_in_ref[p * short : (p + 1) * short, :], ((1,), (1,))).astype(BF16)
        put = one_hot(iota(shape, 0) == short_row(capacity, iota(shape, 1), p))
        term = dot(put, piece)
        back = term if back is None else back + term
    back_ref[...] = back.astype(BF16)
    width = own_ref.shape[1]
    me = place_ref[0]
    for ref, step in ((own_ref, 0), (up_ref, 1), (down_ref, parts - 1)):
        part = lax.rem(me + step, parts)
        ref[...] = hold_ref[:, pl.ds(pl.multiple_of(part * width, width), width)]


def weight_kernel(capacity, *refs):
    out_ref = refs[-1]
    half = (len(refs) - 1) // 2
    short = refs[0].shape[1]
    for p in range(PIECES):
        total = None
        for rows_ref, grad_ref in zip(refs[:half], refs[half:-1], strict=True):
            term = dot(whole_piece(capacity, rows_ref[...], p), grad_ref[...], ((0,), (0,)))
            total = term if total is None else total + term
        out_ref[p * short : (p + 1) * short, :] = total.astype(BF16)


VMEM = pl.BlockSpec(memory_space=pltpu.VMEM)
SMEM = pl.BlockSpec(memory_space=pltpu.SMEM)


def call(kernel, outs, args, specs=None, scratch=(), flops=10**9, moved=4 * 10**6):
    many = isinstance(outs, tuple)
    return pl.pallas_call(
        kernel,
        out_shape=outs,
        in_specs=specs or [VMEM] * len(args),
        out_specs=(VMEM,) * len(outs) if many else VMEM,
        scratch_shapes=list(scratch),
        compiler_params=pltpu.CompilerParams(vmem_limit_bytes=40 * 2**20),
        cost_estimate=pl.CostEstimate(flops=flops, bytes_accessed=moved, transcendentals=0),
    )(*args)


def body(saved_b, route_b, gate_b, grad_y_b, w_in, w_out):
    experts = lax.axis_size("expert")
    parts = lax.axis_size("dp")
    tokens, width = saved_b.shape[1:]
    hidden = w_in.shape[3]
    capacity = max(2, tokens * 5 // (4 * experts))
    count, short = experts * capacity * PIECES, width // PIECES
    table = jax.ShapeDtypeStruct((count, short), BF16)
    route, weight_in, weight_out = route_b[0], w_in[0, 0], w_out[0, 0]

    def exchange(rows):
        return lax.all_to_all(rows, "expert", split_axis=0, concat_axis=0, tiled=True)

    arrived = passed_along(grad_y_b, "segment", -1)[0]
    send_x = call(functools.partial(dispatch_x_kernel, capacity, experts), table, (route, saved_b[0]))
    recv_x = exchange(send_x)
    send_g = call(functools.partial(dispatch_g_kernel, capacity, experts), table, (route, gate_b[0], arrived))
    recv_g = exchange(send_g)
    x_from_below = passed_along(recv_x, "dp", 1)
    x_from_above = passed_along(recv_x, "dp", -1)
    pre = call(
        functools.partial(pre_kernel, capacity),
        jax.ShapeDtypeStruct((experts * capacity, hidden), F32),
        (recv_x, weight_in),
    )
    slim = jax.ShapeDtypeStruct((experts * capacity, hidden // parts), BF16)
    me = lax.axis_index("dp").astype(jnp.int32).reshape(1)
    back, own, up, down = call(
        functools.partial(expert_kernel, capacity, parts),
        (table, slim, slim, slim),
        (me, recv_g, pre, weight_in, weight_out),
        specs=[SMEM] + [VMEM] * 4,
        scratch=[pltpu.VMEM((experts * capacity, hidden), BF16)],
    )
    home = exchange(back)
    g_from_below = passed_along(up, "dp", 1)
    g_from_above = passed_along(down, "dp", -1)
    grad_x = call(
        functools.partial(combine_kernel, capacity),
        jax.ShapeDtypeStruct((tokens, width), BF16),
        (route, home),
    )
    grad_in = call(
        functools.partial(weight_kernel, capacity),
        jax.ShapeDtypeStruct((width, hidden // parts), BF16),
        (recv_x, x_from_below, x_from_above, own, g_from_below, g_from_above),
    )
    return (grad_x[None], grad_in[None, None])


def solution(mesh):
    return jax.shard_map(
        body,
        mesh=mesh,
        in_specs=(
            P("segment", ("dp", "expert"), None),
            P("segment", ("dp", "expert"), None),
            P("segment", ("dp", "expert"), None),
            P("segment", ("dp", "expert"), None),
            P("segment", "expert", None, None),
            P("segment", "expert", None, None),
        ),
        out_specs=(P("segment", ("dp", "expert"), None), P("segment", "expert", None, "dp")),
        check_vma=False,
    )
```

time: 231 us -> 163 us (0.71)
  the two profiles are of different devices: /device:TPU:79 before, /device:TPU:110 now
where the time goes in v1:
time: 163 us; the launch traced here: 162 us
  waiting for transfers between devices  86.9 us (53%)
  starting transfers between devices  48.9 us (30%)
  Pallas kernels  17 us (10%)
  local copies, waits for them, and re-layouts  8.14 us (5%)
    ppermute x5, waiting for transfers between devices, passed_along(): return lax.ppermute(value, axis, pairs)  70.1 us
    all_to_all x3, starting transfers between devices, exchange(): lax.all_to_all(rows, 'expert', split_axis=0, concat_axis=0, tiled=True)  25.2 us
    ppermute x5, starting transfers between devices, passed_along(): return lax.ppermute(value, axis, pairs)  23.7 us
    pallas_call x6, Pallas kernels, call(): pl.pallas_call(kernel, out_shape=outs, in_specs=specs or [VMEM] * len(arg...  17 us
    all_to_all x3, waiting for transfers between devices, exchange(): lax.all_to_all(rows, 'expert', split_axis=0, concat_axis=0, tiled=True)  16.8 us
    unnamed x18, local copies, waits for them, and re-layouts  7.26 us
  transfers between devices with their start and end apart: 8, of which 4 were waited for; matrix products, arithmetic and copies ran while one was open for 0% of the time, Pallas kernels for 6%

profile of v1, /device:TPU:110, one launch (start us, length us, event | category | flops | bytes accessed | tf_op | source)
XLA Modules:
  0.0 161.7 jit_solution(17622004181029203167)
XLA Ops:
  0.6 0.8 copy.11.route_ref
  1.4 1.0 copy-done.7
  2.4 0.8 shard_map.78
  3.2 0.8 copy-done.6
  4.1 9.6 %all-to-all-start.1 = ((bf16[16,40,512]{2,1,0:T(8,128)(2,1)}), bf16[16,40,512]{2,1,0:T(8,128)(2,1)}, u32[]{:S(2)}, u32[]{:S(2)}) async-start(bf16[16,40,512]{2,1,0:T(8,128)(2,1)} %bitcast.21), calls=%async_computation.1 | async-start | bytes 1310720 | tf_op jit(solution)/shard_map/all_to_all | solution.py:176
  13.7 0.2 collective-permute-start
  13.9 0.1 copy.9.gate_ref
  14.0 6.9 %collective-permute-done = bf16[1,128,2048]{2,1,0:T(8,128)(2,1)} collective-permute-done((bf16[1,128,2048]{2,1,0:T(8,128)(2,1)}, bf16[1,128,2048]{2,1,0:T(8,128)(2,1)}, u32[]{:S(2)}, u32[]{:S(2)}) %collective-permute-start) | collective-permute-done | bytes 524320 | tf_op jit(solution)/shard_map/ppermute | solution.py:18
  20.9 1.8 %shard_map.77 = bf16[640,512]{1,0:T(8,128)(2,1)S(1)} custom-call(s32[128,1]{1,0:T(8,128)S(1)} %copy.11.route_ref, f32[128,1]{1,0:T(8,128)S(1)} %copy.9.gate_ref, bf16[128,2048]{1,0:T(8,128)(2,1)} %bitcast.3.values_ref), custom_call_target="tpu_custom_call" | custom-call | flops 1000000000 | bytes 4000000 | tf_op jit(solution)/shard_map/pallas_call | solution.py:154
  22.7 0.0 copy-start.5
  22.7 0.8 copy-done.5
  23.6 5.6 %all-to-all-done.1 = bf16[16,40,512]{2,1,0:T(8,128)(2,1)} async-done(((bf16[16,40,512]{2,1,0:T(8,128)(2,1)}), bf16[16,40,512]{2,1,0:T(8,128)(2,1)}, u32[]{:S(2)}, u32[]{:S(2)}) %all-to-all-start.1) | async-done | bytes 655392 | tf_op jit(solution)/shard_map/all_to_all | solution.py:176
  29.2 8.1 %all-to-all-start = ((bf16[16,40,512]{2,1,0:T(8,128)(2,1)}), bf16[16,40,512]{2,1,0:T(8,128)(2,1)}, u32[]{:S(2)}, u32[]{:S(2)}) async-start(bf16[16,40,512]{2,1,0:T(8,128)(2,1)} %bitcast.20), calls=%async_computation | async-start | bytes 1310720 | tf_op jit(solution)/shard_map/all_to_all | solution.py:176
  37.3 2.7 %shard_map.79.pre_ref = f32[160,768]{1,0:T(8,128)S(1)} custom-call(bf16[640,512]{1,0:T(8,128)(2,1)} %bitcast.8.rows_ref.refs_0_, bf16[2048,768]{1,0:T(8,128)(2,1)S(1)} %bitcast.15), custom_call_target="tpu_custom_call" | custom-call | flops 1000000000 | bytes 4000000 | tf_op jit(solution)/shard_map/pallas_call | solution.py:154
  40.0 0.0 copy-start.2
  40.0 0.8 copy-done.2
  40.7 11.2 %all-to-all-done = bf16[16,40,512]{2,1,0:T(8,128)(2,1)} async-done(((bf16[16,40,512]{2,1,0:T(8,128)(2,1)}), bf16[16,40,512]{2,1,0:T(8,128)(2,1)}, u32[]{:S(2)}, u32[]{:S(2)}) %all-to-all-start) | async-done | bytes 655392 | tf_op jit(solution)/shard_map/all_to_all | solution.py:176
  52.0 1.9 %copy-done.1 = bf16[1,1,768,2048]{3,2,1,0:T(8,128)(2,1)S(1)} copy-done((bf16[1,1,768,2048]{3,2,1,0:T(8,128)(2,1)S(1)}, bf16[1,1,768,2048]{3,2,1,0:T(8,128)(2,1)}, u32[]{:S(2)}) %copy-start.1) | copy-done | bytes 3145752
  53.9 1.0 copy-done.3
  54.9 4.7 %shard_map.80 = (bf16[640,512]{1,0:T(8,128)(2,1)S(1)}, bf16[160,256]{1,0:T(8,128)(2,1)S(1)}, bf16[160,256]{1,0:T(8,128)(2,1)S(1)}, bf16[160,256]{1,0:T(8,128)(2,1)S(1)}) custom-call(s32[1]{0:T(128)} %bitcast.1.place_ref, bf16[640,512]{1,0:T(8,128)(2,1)} %bitcast.5.rows_ref, f32[160,768]{1,0:T(8,128)S(1)} %copy-done.3, bf16[2048,768]{1,0:T(8,128)(2,1)S(1)} %bitcast.16, ...), custom_call_target="tpu_custom_call" | custom-call | flops 1000000000 | bytes 4000000 | tf_op jit(solution)/shard_map/pallas_call | solution.py:154
  59.6 0.8 copy-done.4
  60.4 7.5 %all-to-all-start.2 = ((bf16[16,40,512]{2,1,0:T(8,128)(2,1)}), bf16[16,40,512]{2,1,0:T(8,128)(2,1)S(1)}, u32[]{:S(2)}, u32[]{:S(2)}) async-start(bf16[16,40,512]{2,1,0:T(8,128)(2,1)} %bitcast.19), calls=%async_computation.2 | async-start | bytes 1310720 | tf_op jit(solution)/shard_map/all_to_all | solution.py:176
  67.9 11.9 %collective-permute-start.2 = (bf16[640,512]{1,0:T(8,128)(2,1)}, bf16[640,512]{1,0:T(8,128)(2,1)S(1)}, u32[]{:S(2)}, u32[]{:S(2)}) collective-permute-start(bf16[640,512]{1,0:T(8,128)(2,1)} %bitcast.8.rows_ref.refs_0_), channel_id=1, source_target_pairs={{0,32},{16,0},{32,16},{1,33},{17,1},{33,17},{2,34},{18,2},{34,18},... | collective-permute-start | bytes 1966088 | tf_op jit(solution)/shard_map/ppermute | solution.py:18
  79.8 1.9 %collective-permute-start.1 = (bf16[640,512]{1,0:T(8,128)(2,1)}, bf16[640,512]{1,0:T(8,128)(2,1)S(1)}, u32[]{:S(2)}, u32[]{:S(2)}) collective-permute-start(bf16[640,512]{1,0:T(8,128)(2,1)} %bitcast.8.rows_ref.refs_0_), channel_id=1, source_target_pairs={{0,16},{16,32},{32,0},{1,17},{17,33},{33,1},{2,18},{18,34},{34,2},... | collective-permute-start | bytes 1966088 | tf_op jit(solution)/shard_map/ppermute | solution.py:18
  81.7 6.6 %collective-permute-start.3 = (bf16[160,256]{1,0:T(8,128)(2,1)S(1)}, bf16[160,256]{1,0:T(8,128)(2,1)S(1)}, u32[]{:S(2)}, u32[]{:S(2)}) collective-permute-start(bf16[160,256]{1,0:T(8,128)(2,1)S(1)} %get-tuple-element.8), channel_id=1, source_target_pairs={{0,16},{16,32},{32,0},{1,17},{17,33},{33,1},{2,18},{18,34},{34,2},... | collective-permute-start | bytes 245768 | tf_op jit(solution)/shard_map/ppermute | solution.py:18
  88.3 3.2 %collective-permute-start.4 = (bf16[160,256]{1,0:T(8,128)(2,1)S(1)}, bf16[160,256]{1,0:T(8,128)(2,1)S(1)}, u32[]{:S(2)}, u32[]{:S(2)}) collective-permute-start(bf16[160,256]{1,0:T(8,128)(2,1)S(1)} %get-tuple-element.9), channel_id=1, source_target_pairs={{0,32},{16,0},{32,16},{1,33},{17,1},{33,17},{2,34},{18,2},{34,18},... | collective-permute-start | bytes 245768 | tf_op jit(solution)/shard_map/ppermute | solution.py:18
  91.5 63.2 %collective-permute-done.3.refs_4_ = bf16[160,256]{1,0:T(8,128)(2,1)S(1)} collective-permute-done((bf16[160,256]{1,0:T(8,128)(2,1)S(1)}, bf16[160,256]{1,0:T(8,128)(2,1)S(1)}, u32[]{:S(2)}, u32[]{:S(2)}) %collective-permute-start.3) | collective-permute-done | bytes 81952 | tf_op jit(solution)/shard_map/ppermute | solution.py:18
  154.6 0.0 collective-permute-done.4.refs_5_
  154.6 0.0 collective-permute-done.2.refs_2_
  154.6 0.0 collective-permute-done.1.refs_1_
  154.6 5.3 %shard_map.82 = bf16[2048,256]{1,0:T(8,128)(2,1)} custom-call(bf16[640,512]{1,0:T(8,128)(2,1)} %bitcast.8.rows_ref.refs_0_, bf16[640,512]{1,0:T(8,128)(2,1)S(1)} %collective-permute-done.1.refs_1_, bf16[640,512]{1,0:T(8,128)(2,1)S(1)} %collective-permute-done.2.refs_2_, bf16[160,256]{1,0:T(8,128)(2,1)S(1)} %get-tuple-element.7.refs_3_, ...), custom_call_target="tpu_custom_call" | custom-call | flops 1000000000 | bytes 4000000 | tf_op jit(solution)/shard_map/pallas_call | solution.py:154
  160.0 1.8 %shard_map.81 = bf16[128,2048]{1,0:T(8,128)(2,1)} custom-call(s32[128,1]{1,0:T(8,128)S(1)} %copy.11.route_ref, bf16[640,512]{1,0:T(8,128)(2,1)S(1)} %bitcast.18), custom_call_target="tpu_custom_call" | custom-call | flops 1000000000 | bytes 4000000 | tf_op jit(solution)/shard_map/pallas_call | solution.py:154
  (10 shorter events, 0.0 us)
Async XLA Ops:
  0.6 13.3 %copy-start.8 = (f32[1,128,1]{1,2,0:T(1,128)S(1)}, f32[1,128,1]{1,2,0:T(1,128)}, u32[]{:S(2)}) copy-start(f32[1,128,1]{1,2,0:T(1,128)} %param.8) | copy-start | bytes 1540
  1.4 1.0 copy-start.7
  3.2 0.9 copy-start.6
  4.1 33.2 %copy-start = (bf16[1,1,2048,768]{3,2,1,0:T(8,128)(2,1)S(1)}, bf16[1,1,2048,768]{3,2,1,0:T(8,128)(2,1)}, u32[]{:S(2)}) copy-start(bf16[1,1,2048,768]{3,2,1,0:T(8,128)(2,1)} %param.10) | copy-start | bytes 9437188
  4.1 25.1 %all-to-all-start.1 = ((bf16[16,40,512]{2,1,0:T(8,128)(2,1)}), bf16[16,40,512]{2,1,0:T(8,128)(2,1)}, u32[]{:S(2)}, u32[]{:S(2)}) async-start(bf16[16,40,512]{2,1,0:T(8,128)(2,1)} %bitcast.21), calls=%async_computation.1 | async-start | bytes 1310720 | tf_op jit(solution)/shard_map/all_to_all | solution.py:176
  13.7 7.2 %collective-permute-start = (bf16[1,128,2048]{2,1,0:T(8,128)(2,1)}, bf16[1,128,2048]{2,1,0:T(8,128)(2,1)}, u32[]{:S(2)}, u32[]{:S(2)}) collective-permute-start(bf16[1,128,2048]{2,1,0:T(8,128)(2,1)} %param.9), channel_id=1, source_target_pairs={{0,720},{48,0},{96,48},{144,96},{192,144},{240,192},{288,240},{336... | collective-permute-start | bytes 1572872 | tf_op jit(solution)/shard_map/ppermute | solution.py:18
  22.7 0.8 copy-start.5
  29.2 22.8 %all-to-all-start = ((bf16[16,40,512]{2,1,0:T(8,128)(2,1)}), bf16[16,40,512]{2,1,0:T(8,128)(2,1)}, u32[]{:S(2)}, u32[]{:S(2)}) async-start(bf16[16,40,512]{2,1,0:T(8,128)(2,1)} %bitcast.20), calls=%async_computation | async-start | bytes 1310720 | tf_op jit(solution)/shard_map/all_to_all | solution.py:176
  40.0 0.8 copy-start.2
  52.0 1.9 %copy-start.1 = (bf16[1,1,768,2048]{3,2,1,0:T(8,128)(2,1)S(1)}, bf16[1,1,768,2048]{3,2,1,0:T(8,128)(2,1)}, u32[]{:S(2)}) copy-start(bf16[1,1,768,2048]{3,2,1,0:T(8,128)(2,1)} %param.11) | copy-start | bytes 9437188
  53.9 1.0 copy-start.3
  59.6 0.9 copy-start.4
  60.4 99.5 %all-to-all-start.2 = ((bf16[16,40,512]{2,1,0:T(8,128)(2,1)}), bf16[16,40,512]{2,1,0:T(8,128)(2,1)S(1)}, u32[]{:S(2)}, u32[]{:S(2)}) async-start(bf16[16,40,512]{2,1,0:T(8,128)(2,1)} %bitcast.19), calls=%async_computation.2 | async-start | bytes 1310720 | tf_op jit(solution)/shard_map/all_to_all | solution.py:176
  67.9 86.7 %collective-permute-start.2 = (bf16[640,512]{1,0:T(8,128)(2,1)}, bf16[640,512]{1,0:T(8,128)(2,1)S(1)}, u32[]{:S(2)}, u32[]{:S(2)}) collective-permute-start(bf16[640,512]{1,0:T(8,128)(2,1)} %bitcast.8.rows_ref.refs_0_), channel_id=1, source_target_pairs={{0,32},{16,0},{32,16},{1,33},{17,1},{33,17},{2,34},{18,2},{34,18},... | collective-permute-start | bytes 1966088 | tf_op jit(solution)/shard_map/ppermute | solution.py:18
  79.8 74.9 %collective-permute-start.1 = (bf16[640,512]{1,0:T(8,128)(2,1)}, bf16[640,512]{1,0:T(8,128)(2,1)S(1)}, u32[]{:S(2)}, u32[]{:S(2)}) collective-permute-start(bf16[640,512]{1,0:T(8,128)(2,1)} %bitcast.8.rows_ref.refs_0_), channel_id=1, source_target_pairs={{0,16},{16,32},{32,0},{1,17},{17,33},{33,1},{2,18},{18,34},{34,2},... | collective-permute-start | bytes 1966088 | tf_op jit(solution)/shard_map/ppermute | solution.py:18
  81.7 72.9 %collective-permute-start.3 = (bf16[160,256]{1,0:T(8,128)(2,1)S(1)}, bf16[160,256]{1,0:T(8,128)(2,1)S(1)}, u32[]{:S(2)}, u32[]{:S(2)}) collective-permute-start(bf16[160,256]{1,0:T(8,128)(2,1)S(1)} %get-tuple-element.8), channel_id=1, source_target_pairs={{0,16},{16,32},{32,0},{1,17},{17,33},{33,1},{2,18},{18,34},{34,2},... | collective-permute-start | bytes 245768 | tf_op jit(solution)/shard_map/ppermute | solution.py:18
  88.3 66.3 %collective-permute-start.4 = (bf16[160,256]{1,0:T(8,128)(2,1)S(1)}, bf16[160,256]{1,0:T(8,128)(2,1)S(1)}, u32[]{:S(2)}, u32[]{:S(2)}) collective-permute-start(bf16[160,256]{1,0:T(8,128)(2,1)S(1)} %get-tuple-element.9), channel_id=1, source_target_pairs={{0,32},{16,0},{32,16},{1,33},{17,1},{33,17},{2,34},{18,2},{34,18},... | collective-permute-start | bytes 245768 | tf_op jit(solution)/shard_map/ppermute | solution.py:18

commit v2 on v1

v2 whole, which is shorter than its diff:
```python
import functools

import jax
import jax.numpy as jnp
from jax import lax
from jax.experimental import pallas as pl
from jax.experimental.pallas import tpu as pltpu
from jax.sharding import PartitionSpec as P

PIECES = 4
F32 = jnp.float32
BF16 = jnp.bfloat16


def passed_along(value, axis, steps):
    count = lax.axis_size(axis)
    pairs = [(source, (source + steps) % count) for source in range(count)]
    return lax.ppermute(value, axis, pairs)


def silu_grad(value):
    sigma = jax.nn.sigmoid(value)
    return sigma * (1.0 + value * (1.0 - sigma))


def iota(shape, dim):
    return lax.broadcasted_iota(jnp.int32, shape, dim)


def one_hot(condition):
    return jnp.where(condition, 1.0, 0.0).astype(BF16)


def dot(a, b, contract=((1,), (0,))):
    return lax.dot_general(a, b, (contract, ((), ())), preferred_element_type=F32)


def first_short_row(route, rank, capacity, piece):
    main = capacity // 8 * 8
    rest = capacity - main
    inside = jnp.where(rank < main, piece * main + rank, PIECES * main + piece * rest + rank - main)
    return route * (PIECES * capacity) + inside


def slots_along_lanes(route, experts):
    tokens = route.shape[0]
    square = (tokens, tokens)
    lane_route = jnp.sum(
        jnp.where(iota(square, 0) == iota(square, 1), route.astype(F32), 0.0), axis=0, keepdims=True
    )
    named = one_hot(iota((experts, tokens), 0).astype(F32) == lane_route)
    before = dot(named, one_hot(iota(square, 0) < iota(square, 1)))
    rank = jnp.sum(before * named.astype(F32), axis=0, keepdims=True)
    return lane_route.astype(jnp.int32), rank.astype(jnp.int32)


def slots_along_sublanes(route):
    tokens = route.shape[0]
    square = (tokens, tokens)
    named = one_hot(iota(square, 1) == route)
    before = dot(one_hot(iota(square, 1) < iota(square, 0)), named)
    return jnp.sum(before * named.astype(F32), axis=1, keepdims=True).astype(jnp.int32)


def place(route, values, capacity, experts, rows):
    tokens, width = values.shape
    short = width // PIECES
    lane_route, rank = slots_along_lanes(route, experts)
    at = iota((rows, tokens), 0)
    table = jnp.concatenate(
        [one_hot(at == first_short_row(lane_route, rank, capacity, p)) for p in range(PIECES)], axis=1
    )
    stacked = jnp.concatenate([values[:, p * short : (p + 1) * short] for p in range(PIECES)], axis=0)
    return dot(table, stacked).astype(BF16)


def dispatch_x_kernel(capacity, experts, route_ref, values_ref, out_ref):
    out_ref[...] = place(route_ref[...], values_ref[...], capacity, experts, out_ref.shape[0])


def dispatch_g_kernel(capacity, experts, route_ref, gate_ref, values_ref, out_ref):
    scaled = (gate_ref[...] * values_ref[...].astype(F32)).astype(BF16)
    out_ref[...] = place(route_ref[...], scaled, capacity, experts, out_ref.shape[0])


def combine_kernel(capacity, route_ref, rows_ref, _after_ref, out_ref):
    route = route_ref[...]
    rank = slots_along_sublanes(route)
    rows = rows_ref[...]
    count, short = rows.shape
    at = iota((route.shape[0], count), 1)
    for p in range(PIECES):
        table = one_hot(at == first_short_row(route, rank, capacity, p))
        out_ref[:, p * short : (p + 1) * short] = dot(table, rows).astype(BF16)


def rest_table(chunks, rest, piece, dim):
    long, slim = chunks * PIECES * rest, chunks * rest
    shape = (slim, long) if dim else (long, slim)
    row, at = iota(shape, 1 - dim), iota(shape, dim)
    chunk = row >> (rest.bit_length() - 1)
    return one_hot(at == chunk * (PIECES * rest) + piece * rest + (row & (rest - 1)))


def whole_piece(capacity, ref, piece, packed):
    main = capacity // 8 * 8
    rest = capacity - main
    chunks, short = ref.shape[0], ref.shape[2]
    first = ref[:, piece * main : (piece + 1) * main, :].reshape(chunks * main, short)
    last = dot(rest_table(chunks, rest, piece, 1), packed).astype(BF16)
    return first, last


def packed_rest(capacity, ref):
    main = capacity // 8 * 8
    rest = capacity - main
    return ref[:, PIECES * main :, :].reshape(ref.shape[0] * PIECES * rest, ref.shape[2])


def joined(capacity, ref, piece, packed):
    return jnp.concatenate(whole_piece(capacity, ref, piece, packed), axis=0)


def pre_kernel(capacity, rows_ref, w_in_ref, pre_ref):
    short = rows_ref.shape[2]
    packed = packed_rest(capacity, rows_ref)
    total = None
    for p in range(PIECES):
        term = dot(joined(capacity, rows_ref, p, packed), w_in_ref[p * short : (p + 1) * short, :])
        total = term if total is None else total + term
    pre_ref[...] = total


def expert_kernel(capacity, parts, place_ref, rows_hbm, pre_hbm, w_in_hbm, w_out_hbm,
                  back_ref, own_ref, up_ref, down_ref,
                  hold_ref, held_ref, rows_ref, pre_ref, w_in_ref, w_out_ref, sems, in_sems):
    chunks, short = rows_ref.shape[0], rows_ref.shape[2]
    main = capacity // 8 * 8
    rest = capacity - main
    fetch_rows = pltpu.make_async_copy(rows_hbm, rows_ref, in_sems.at[0])
    fetch_rows.start()
    fetches = []
    for p in range(PIECES):
        at = pl.ds(p * short, short)
        fetches.append(pltpu.make_async_copy(w_out_hbm.at[:, at], w_out_ref.at[p], in_sems.at[2 + p]))
        fetches[-1].start()
    fetch_pre = pltpu.make_async_copy(pre_hbm, pre_ref, in_sems.at[1])
    fetch_pre.start()
    for p in range(PIECES):
        at = pl.ds(p * short, short)
        fetches.append(pltpu.make_async_copy(w_in_hbm.at[at, :], w_in_ref.at[p], in_sems.at[2 + PIECES + p]))
        fetches[-1].start()
    fetch_rows.wait()
    packed = packed_rest(capacity, rows_ref)
    total = None
    for p in range(PIECES):
        whole = joined(capacity, rows_ref, p, packed)
        fetches[p].wait()
        term = dot(whole, w_out_ref[p], ((1,), (1,)))
        total = term if total is None else total + term
    fetch_pre.wait()
    grad_pre = (total * silu_grad(pre_ref[...])).astype(BF16)
    hold_ref[...] = grad_pre
    width = own_ref.shape[1]
    me = place_ref[0]
    copies = []
    for i, (ref, step) in enumerate(((up_ref, 1), (down_ref, parts - 1), (own_ref, 0))):
        at = pl.ds(pl.multiple_of(lax.rem(me + step, parts) * width, width), width)
        copies.append(pltpu.make_async_copy(hold_ref.at[:, at], ref, sems.at[i]))
        copies[-1].start()
    last = None
    for p in range(PIECES):
        fetches[PIECES + p].wait()
        piece = dot(grad_pre, w_in_ref[p], ((1,), (1,))).astype(BF16)
        held_ref[:, p * main : (p + 1) * main, :] = piece[: chunks * main].reshape(chunks, main, short)
        at = pl.ds(p * main, main)
        copies.append(pltpu.make_async_copy(held_ref.at[:, at, :], back_ref.at[:, at, :], sems.at[3 + p]))
        copies[-1].start()
        term = dot(rest_table(chunks, rest, p, 0), piece[chunks * main :])
        last = term if last is None else last + term
    held_ref[:, PIECES * main :, :] = last.astype(BF16).reshape(chunks, PIECES * rest, short)
    at = pl.ds(PIECES * main, PIECES * rest)
    copies.append(pltpu.make_async_copy(held_ref.at[:, at, :], back_ref.at[:, at, :], sems.at[3 + PIECES]))
    copies[-1].start()
    for copy in copies:
        copy.wait()


def weight_kernel(capacity, *refs):
    out_ref, done_ref = refs[-2:]
    refs = refs[:-1]
    half = (len(refs) - 1) // 2
    done_ref[...] = jnp.zeros(done_ref.shape, F32)
    chunks, _, short = refs[0].shape
    main = capacity // 8 * 8
    grads = []
    for ref in refs[half:-1]:
        grads += [ref[: chunks * main], ref[chunks * main :]]
    grads = jnp.concatenate(grads, axis=0)
    rests = [packed_rest(capacity, ref) for ref in refs[:half]]
    for p in range(PIECES):
        rows = []
        for ref, packed in zip(refs[:half], rests, strict=True):
            rows += list(whole_piece(capacity, ref, p, packed))
        total = dot(jnp.concatenate(rows, axis=0), grads, ((0,), (0,)))
        out_ref[p * short : (p + 1) * short, :] = total.astype(BF16)


VMEM = pl.BlockSpec(memory_space=pltpu.VMEM)
SMEM = pl.BlockSpec(memory_space=pltpu.SMEM)
ANY = pl.BlockSpec(memory_space=pl.ANY)


def in_hbm(value):
    return pltpu.with_memory_space_constraint(value, pltpu.HBM)


def call(kernel, outs, args, specs=None, out_spec=VMEM, scratch=(), flops=10**9, moved=4 * 10**6):
    many = isinstance(outs, tuple)
    return pl.pallas_call(
        kernel,
        out_shape=outs,
        in_specs=specs or [VMEM] * len(args),
        out_specs=(out_spec,) * len(outs) if many else out_spec,
        scratch_shapes=list(scratch),
        compiler_params=pltpu.CompilerParams(vmem_limit_bytes=24 * 2**20),
        cost_estimate=pl.CostEstimate(flops=flops, bytes_accessed=moved, transcendentals=0),
    )(*args)


def body(saved_b, route_b, gate_b, grad_y_b, w_in, w_out):
    experts = lax.axis_size("expert")
    parts = lax.axis_size("dp")
    tokens, width = saved_b.shape[1:]
    hidden = w_in.shape[3]
    capacity = max(2, tokens * 5 // (4 * experts))
    chunk, short = PIECES * capacity, width // PIECES
    count = experts * chunk
    table = jax.ShapeDtypeStruct((count, short), BF16)
    route, weight_in, weight_out = route_b[0], w_in[0, 0], w_out[0, 0]

    def exchange(rows):
        return lax.all_to_all(rows, "expert", split_axis=0, concat_axis=0, tiled=True)

    arrived = passed_along(grad_y_b, "segment", -1)[0]
    send_x = call(functools.partial(dispatch_x_kernel, capacity, experts), table, (route, saved_b[0]))
    recv_x = exchange(send_x.reshape(experts, chunk, short))
    send_g = call(functools.partial(dispatch_g_kernel, capacity, experts), table, (route, gate_b[0], arrived))
    recv_g = exchange(send_g.reshape(experts, chunk, short))
    x_from_below = passed_along(recv_x, "dp", 1)
    x_from_above = passed_along(recv_x, "dp", -1)
    pre = call(
        functools.partial(pre_kernel, capacity),
        pltpu.HBM((experts * capacity, hidden), F32),
        (recv_x, weight_in),
        flops=1000,
        moved=1000,
    )
    columns = pltpu.HBM((experts * capacity, hidden // parts), BF16)
    me = lax.axis_index("dp").astype(jnp.int32).reshape(1)
    back, own, up, down = call(
        functools.partial(expert_kernel, capacity, parts),
        (pltpu.HBM((experts, chunk, short), BF16), columns, columns, columns),
        (me, in_hbm(recv_g), in_hbm(pre), in_hbm(weight_in), in_hbm(weight_out)),
        specs=[SMEM, ANY, ANY, ANY, ANY],
        out_spec=ANY,
        scratch=[
            pltpu.VMEM((experts * capacity, hidden), BF16),
            pltpu.VMEM((experts, chunk, short), BF16),
            pltpu.VMEM((experts, chunk, short), BF16),
            pltpu.VMEM((experts * capacity, hidden), F32),
            pltpu.VMEM((PIECES, short, hidden), BF16),
            pltpu.VMEM((PIECES, hidden, short), BF16),
            pltpu.SemaphoreType.DMA((4 + PIECES,)),
            pltpu.SemaphoreType.DMA((2 + 2 * PIECES,)),
        ],
        flops=1000,
        moved=1000,
    )
    home = exchange(back)
    g_from_below = passed_along(up, "dp", 1)
    g_from_above = passed_along(down, "dp", -1)
    grad_in, done = call(
        functools.partial(weight_kernel, capacity),
        (jax.ShapeDtypeStruct((width, hidden // parts), BF16), jax.ShapeDtypeStruct((8, 128), F32)),
        (recv_x, x_from_below, x_from_above, own, g_from_below, g_from_above),
        flops=5*10**12,
    )
    grad_x = call(
        functools.partial(combine_kernel, capacity),
        jax.ShapeDtypeStruct((tokens, width), BF16),
        (route, home.reshape(count, short), done),
        flops=1000,
        moved=1000,
    )
    return (grad_x[None], grad_in[None, None])


def solution(mesh):
    return jax.shard_map(
        body,
        mesh=mesh,
        in_specs=(
            P("segment", ("dp", "expert"), None),
            P("segment", ("dp", "expert"), None),
            P("segment", ("dp", "expert"), None),
            P("segment", ("dp", "expert"), None),
            P("segment", "expert", None, None),
            P("segment", "expert", None, None),
        ),
        out_specs=(P("segment", ("dp", "expert"), None), P("segment", "expert", None, "dp")),
        check_vma=False,
    )
```

time: 163 us -> 145 us (0.89)
  the two profiles are of different devices: /device:TPU:110 before, /device:TPU:1 now
where the time goes in v2:
time: 145 us; the launch traced here: 144 us
  waiting for transfers between devices  68.7 us (47%)
  starting transfers between devices  52.2 us (36%)
  Pallas kernels  18 us (12%)
  local copies, waits for them, and re-layouts  4.49 us (3%)
    all_to_all x3, waiting for transfers between devices, exchange(): lax.all_to_all(rows, 'expert', split_axis=0, concat_axis=0, tiled=True)  60.3 us
    ppermute x5, starting transfers between devices, passed_along(): return lax.ppermute(value, axis, pairs)  32.6 us
    all_to_all x3, starting transfers between devices, exchange(): lax.all_to_all(rows, 'expert', split_axis=0, concat_axis=0, tiled=True)  19.6 us
    pallas_call x6, Pallas kernels, call(): pl.pallas_call(kernel, out_shape=outs, in_specs=specs or [VMEM] * len(arg...  18 us
    ppermute x5, waiting for transfers between devices, passed_along(): return lax.ppermute(value, axis, pairs)  8.39 us
    unnamed x12, local copies, waits for them, and re-layouts  3.61 us
  transfers between devices with their start and end apart: 8, of which 5 were waited for; matrix products, arithmetic and copies ran while one was open for 0% of the time, Pallas kernels for 10%

profile of v2, /device:TPU:1, one launch (start us, length us, event | category | flops | bytes accessed | tf_op | source)
XLA Modules:
  0.0 144.2 jit_solution(5799803026931947944)
XLA Ops:
  0.6 0.0 copy-start.5
  0.6 0.8 copy.11.route_ref
  1.4 1.0 copy-done.3
  2.4 0.8 shard_map.78
  3.2 0.0 copy-start.2
  3.2 0.8 copy-done.2
  4.1 10.7 %all-to-all-start.1 = ((bf16[16,40,512]{2,1,0:T(8,128)(2,1)}), bf16[16,40,512]{2,1,0:T(8,128)(2,1)}, u32[]{:S(2)}, u32[]{:S(2)}) async-start(bf16[16,40,512]{2,1,0:T(8,128)(2,1)} %bitcast.15), calls=%async_computation.1 | async-start | bytes 1310720 | tf_op jit(solution)/shard_map/all_to_all | solution.py:243
  14.8 4.4 %collective-permute-start = (bf16[1,128,2048]{2,1,0:T(8,128)(2,1)}, bf16[1,128,2048]{2,1,0:T(8,128)(2,1)}, u32[]{:S(2)}, u32[]{:S(2)}) collective-permute-start(bf16[1,128,2048]{2,1,0:T(8,128)(2,1)} %param.9), channel_id=1, source_target_pairs={{0,720},{48,0},{96,48},{144,96},{192,144},{240,192},{288,240},{336... | collective-permute-start | bytes 1572872 | tf_op jit(solution)/shard_map/ppermute | solution.py:18
  19.2 0.0 copy-done.5
  19.2 0.1 copy.9.gate_ref
  19.3 5.1 %collective-permute-done = bf16[1,128,2048]{2,1,0:T(8,128)(2,1)} collective-permute-done((bf16[1,128,2048]{2,1,0:T(8,128)(2,1)}, bf16[1,128,2048]{2,1,0:T(8,128)(2,1)}, u32[]{:S(2)}, u32[]{:S(2)}) %collective-permute-start) | collective-permute-done | bytes 524320 | tf_op jit(solution)/shard_map/ppermute | solution.py:18
  24.4 1.8 %shard_map.77 = bf16[640,512]{1,0:T(8,128)(2,1)S(1)} custom-call(s32[128,1]{1,0:T(8,128)S(1)} %copy.11.route_ref, f32[128,1]{1,0:T(8,128)S(1)} %copy.9.gate_ref, bf16[128,2048]{1,0:T(8,128)(2,1)} %bitcast.3.values_ref), custom_call_target="tpu_custom_call" | custom-call | flops 1000000000 | bytes 4000000 | tf_op jit(solution)/shard_map/pallas_call | solution.py:220
  26.2 0.0 copy-start.1
  26.2 0.8 copy-done.1
  27.1 5.1 %all-to-all-done.1.rows_ref.refs_0_ = bf16[16,40,512]{2,1,0:T(8,128)(2,1)} async-done(((bf16[16,40,512]{2,1,0:T(8,128)(2,1)}), bf16[16,40,512]{2,1,0:T(8,128)(2,1)}, u32[]{:S(2)}, u32[]{:S(2)}) %all-to-all-start.1) | async-done | bytes 655392 | tf_op jit(solution)/shard_map/all_to_all | solution.py:243
  32.2 4.3 %all-to-all-start = ((bf16[16,40,512]{2,1,0:T(8,128)(2,1)}), bf16[16,40,512]{2,1,0:T(8,128)(2,1)}, u32[]{:S(2)}, u32[]{:S(2)}) async-start(bf16[16,40,512]{2,1,0:T(8,128)(2,1)} %bitcast.14), calls=%async_computation | async-start | bytes 1310720 | tf_op jit(solution)/shard_map/all_to_all | solution.py:243
  36.4 12.7 %collective-permute-start.2 = (bf16[16,40,512]{2,1,0:T(8,128)(2,1)}, bf16[16,40,512]{2,1,0:T(8,128)(2,1)}, u32[]{:S(2)}, u32[]{:S(2)}) collective-permute-start(bf16[16,40,512]{2,1,0:T(8,128)(2,1)} %all-to-all-done.1.rows_ref.refs_0_), channel_id=1, source_target_pairs={{0,32},{16,0},{32,16},{1,33},{17,1},{33,17},{2,34},{18,2},{34,18},... | collective-permute-start | bytes 1966088 | tf_op jit(solution)/shard_map/ppermute | solution.py:18
  49.2 1.9 %collective-permute-start.1 = (bf16[16,40,512]{2,1,0:T(8,128)(2,1)}, bf16[16,40,512]{2,1,0:T(8,128)(2,1)}, u32[]{:S(2)}, u32[]{:S(2)}) collective-permute-start(bf16[16,40,512]{2,1,0:T(8,128)(2,1)} %all-to-all-done.1.rows_ref.refs_0_), channel_id=1, source_target_pairs={{0,16},{16,32},{32,0},{1,17},{17,33},{33,1},{2,18},{18,34},{34,2},... | collective-permute-start | bytes 1966088 | tf_op jit(solution)/shard_map/ppermute | solution.py:18
  51.2 2.8 %shard_map.79.pre_hbm = f32[160,768]{1,0:T(8,128)} custom-call(bf16[16,40,512]{2,1,0:T(8,128)(2,1)} %all-to-all-done.1.rows_ref.refs_0_, bf16[2048,768]{1,0:T(8,128)(2,1)S(1)} %bitcast.13), custom_call_target="tpu_custom_call" | custom-call | flops 1000 | bytes 1000 | tf_op jit(solution)/shard_map/pallas_call | solution.py:220
  54.0 43.0 %all-to-all-done.rows_hbm = bf16[16,40,512]{2,1,0:T(8,128)(2,1)} async-done(((bf16[16,40,512]{2,1,0:T(8,128)(2,1)}), bf16[16,40,512]{2,1,0:T(8,128)(2,1)}, u32[]{:S(2)}, u32[]{:S(2)}) %all-to-all-start) | async-done | bytes 655392 | tf_op jit(solution)/shard_map/all_to_all | solution.py:243
  97.0 6.2 %shard_map.80 = (bf16[16,40,512]{2,1,0:T(8,128)(2,1)}, bf16[160,256]{1,0:T(8,128)(2,1)}, bf16[160,256]{1,0:T(8,128)(2,1)}, bf16[160,256]{1,0:T(8,128)(2,1)}) custom-call(s32[1]{0:T(128)} %bitcast.1.place_ref, bf16[16,40,512]{2,1,0:T(8,128)(2,1)} %all-to-all-done.rows_hbm, f32[160,768]{1,0:T(8,128)} %shard_map.79.pre_hbm, bf16[2048,768]{1,0:T(8,128)(2,1)} %bitcast.12, ...), custom_call_target="tpu_custom_call" | custom-call | flops 1000 | bytes 1000 | tf_op jit(solution)/shard_map/pallas_call | solution.py:220
  103.2 11.6 %collective-permute-start.3 = (bf16[160,256]{1,0:T(8,128)(2,1)}, bf16[160,256]{1,0:T(8,128)(2,1)S(1)}, u32[]{:S(2)}, u32[]{:S(2)}) collective-permute-start(bf16[160,256]{1,0:T(8,128)(2,1)} %get-tuple-element.10), channel_id=1, source_target_pairs={{0,16},{16,32},{32,0},{1,17},{17,33},{33,1},{2,18},{18,34},{34,2},... | collective-permute-start | bytes 245768 | tf_op jit(solution)/shard_map/ppermute | solution.py:18
  114.9 1.9 %collective-permute-start.4 = (bf16[160,256]{1,0:T(8,128)(2,1)}, bf16[160,256]{1,0:T(8,128)(2,1)S(1)}, u32[]{:S(2)}, u32[]{:S(2)}) collective-permute-start(bf16[160,256]{1,0:T(8,128)(2,1)} %get-tuple-element.11), channel_id=1, source_target_pairs={{0,32},{16,0},{32,16},{1,33},{17,1},{33,17},{2,34},{18,2},{34,18},... | collective-permute-start | bytes 245768 | tf_op jit(solution)/shard_map/ppermute | solution.py:18
  116.8 4.6 %all-to-all-start.2 = ((bf16[16,40,512]{2,1,0:T(8,128)(2,1)}), bf16[16,40,512]{2,1,0:T(8,128)(2,1)}, u32[]{:S(2)}, u32[]{:S(2)}) async-start(bf16[16,40,512]{2,1,0:T(8,128)(2,1)} %get-tuple-element.8), calls=%async_computation.2 | async-start | bytes 1310720 | tf_op jit(solution)/shard_map/all_to_all | solution.py:243
  121.4 0.0 collective-permute-done.3.refs_4_
  121.5 3.3 %collective-permute-done.4.refs_5_ = bf16[160,256]{1,0:T(8,128)(2,1)S(1)} collective-permute-done((bf16[160,256]{1,0:T(8,128)(2,1)}, bf16[160,256]{1,0:T(8,128)(2,1)S(1)}, u32[]{:S(2)}, u32[]{:S(2)}) %collective-permute-start.4) | collective-permute-done | bytes 81952 | tf_op jit(solution)/shard_map/ppermute | solution.py:18
  124.7 0.0 collective-permute-done.2.refs_2_
  124.7 0.0 collective-permute-done.1.refs_1_
  124.7 0.9 copy-done.4
  125.6 3.6 %shard_map.81 = (bf16[2048,256]{1,0:T(8,128)(2,1)}, f32[8,128]{1,0:T(8,128)S(1)}) custom-call(bf16[16,40,512]{2,1,0:T(8,128)(2,1)} %all-to-all-done.1.rows_ref.refs_0_, bf16[16,40,512]{2,1,0:T(8,128)(2,1)} %collective-permute-done.1.refs_1_, bf16[16,40,512]{2,1,0:T(8,128)(2,1)} %collective-permute-done.2.refs_2_, bf16[160,256]{1,0:T(8,128)(2,1)S(1)} %copy-done.4, ...), custom_call_target="tpu_custom_call" | custom-call | flops 4999999913984 | bytes 4000000 | tf_op jit(solution)/shard_map/pallas_call | solution.py:220
  129.2 12.2 %all-to-all-done.2 = bf16[16,40,512]{2,1,0:T(8,128)(2,1)} async-done(((bf16[16,40,512]{2,1,0:T(8,128)(2,1)}), bf16[16,40,512]{2,1,0:T(8,128)(2,1)}, u32[]{:S(2)}, u32[]{:S(2)}) %all-to-all-start.2) | async-done | bytes 655392 | tf_op jit(solution)/shard_map/all_to_all | solution.py:243
  141.3 2.8 %shard_map.82 = bf16[128,2048]{1,0:T(8,128)(2,1)} custom-call(s32[128,1]{1,0:T(8,128)S(1)} %copy.11.route_ref, bf16[640,512]{1,0:T(8,128)(2,1)} %bitcast.9.rows_ref, f32[8,128]{1,0:T(8,128)S(1)} %get-tuple-element.12._after_ref), custom_call_target="tpu_custom_call" | custom-call | flops 1000 | bytes 1000 | tf_op jit(solution)/shard_map/pallas_call | solution.py:220
  (4 shorter events, 0.0 us)
Async XLA Ops:
  0.6 18.5 %copy-start.5 = (f32[1,128,1]{1,2,0:T(1,128)S(1)}, f32[1,128,1]{1,2,0:T(1,128)}, u32[]{:S(2)}) copy-start(f32[1,128,1]{1,2,0:T(1,128)} %param.8) | copy-start | bytes 1540
  1.4 1.0 copy-start.3
  3.2 0.9 copy-start.2
  4.1 47.1 %copy-start = (bf16[1,1,2048,768]{3,2,1,0:T(8,128)(2,1)S(1)}, bf16[1,1,2048,768]{3,2,1,0:T(8,128)(2,1)}, u32[]{:S(2)}) copy-start(bf16[1,1,2048,768]{3,2,1,0:T(8,128)(2,1)} %param.10) | copy-start | bytes 9437188
  4.1 28.1 %all-to-all-start.1 = ((bf16[16,40,512]{2,1,0:T(8,128)(2,1)}), bf16[16,40,512]{2,1,0:T(8,128)(2,1)}, u32[]{:S(2)}, u32[]{:S(2)}) async-start(bf16[16,40,512]{2,1,0:T(8,128)(2,1)} %bitcast.15), calls=%async_computation.1 | async-start | bytes 1310720 | tf_op jit(solution)/shard_map/all_to_all | solution.py:243
  14.8 9.6 %collective-permute-start = (bf16[1,128,2048]{2,1,0:T(8,128)(2,1)}, bf16[1,128,2048]{2,1,0:T(8,128)(2,1)}, u32[]{:S(2)}, u32[]{:S(2)}) collective-permute-start(bf16[1,128,2048]{2,1,0:T(8,128)(2,1)} %param.9), channel_id=1, source_target_pairs={{0,720},{48,0},{96,48},{144,96},{192,144},{240,192},{288,240},{336... | collective-permute-start | bytes 1572872 | tf_op jit(solution)/shard_map/ppermute | solution.py:18
  26.2 0.8 copy-start.1
  32.2 64.8 %all-to-all-start = ((bf16[16,40,512]{2,1,0:T(8,128)(2,1)}), bf16[16,40,512]{2,1,0:T(8,128)(2,1)}, u32[]{:S(2)}, u32[]{:S(2)}) async-start(bf16[16,40,512]{2,1,0:T(8,128)(2,1)} %bitcast.14), calls=%async_computation | async-start | bytes 1310720 | tf_op jit(solution)/shard_map/all_to_all | solution.py:243
  36.4 88.3 %collective-permute-start.2 = (bf16[16,40,512]{2,1,0:T(8,128)(2,1)}, bf16[16,40,512]{2,1,0:T(8,128)(2,1)}, u32[]{:S(2)}, u32[]{:S(2)}) collective-permute-start(bf16[16,40,512]{2,1,0:T(8,128)(2,1)} %all-to-all-done.1.rows_ref.refs_0_), channel_id=1, source_target_pairs={{0,32},{16,0},{32,16},{1,33},{17,1},{33,17},{2,34},{18,2},{34,18},... | collective-permute-start | bytes 1966088 | tf_op jit(solution)/shard_map/ppermute | solution.py:18
  49.2 75.5 %collective-permute-start.1 = (bf16[16,40,512]{2,1,0:T(8,128)(2,1)}, bf16[16,40,512]{2,1,0:T(8,128)(2,1)}, u32[]{:S(2)}, u32[]{:S(2)}) collective-permute-start(bf16[16,40,512]{2,1,0:T(8,128)(2,1)} %all-to-all-done.1.rows_ref.refs_0_), channel_id=1, source_target_pairs={{0,16},{16,32},{32,0},{1,17},{17,33},{33,1},{2,18},{18,34},{34,2},... | collective-permute-start | bytes 1966088 | tf_op jit(solution)/shard_map/ppermute | solution.py:18
  103.2 18.2 %collective-permute-start.3 = (bf16[160,256]{1,0:T(8,128)(2,1)}, bf16[160,256]{1,0:T(8,128)(2,1)S(1)}, u32[]{:S(2)}, u32[]{:S(2)}) collective-permute-start(bf16[160,256]{1,0:T(8,128)(2,1)} %get-tuple-element.10), channel_id=1, source_target_pairs={{0,16},{16,32},{32,0},{1,17},{17,33},{33,1},{2,18},{18,34},{34,2},... | collective-permute-start | bytes 245768 | tf_op jit(solution)/shard_map/ppermute | solution.py:18
  114.9 9.9 %collective-permute-start.4 = (bf16[160,256]{1,0:T(8,128)(2,1)}, bf16[160,256]{1,0:T(8,128)(2,1)S(1)}, u32[]{:S(2)}, u32[]{:S(2)}) collective-permute-start(bf16[160,256]{1,0:T(8,128)(2,1)} %get-tuple-element.11), channel_id=1, source_target_pairs={{0,32},{16,0},{32,16},{1,33},{17,1},{33,17},{2,34},{18,2},{34,18},... | collective-permute-start | bytes 245768 | tf_op jit(solution)/shard_map/ppermute | solution.py:18
  116.8 24.5 %all-to-all-start.2 = ((bf16[16,40,512]{2,1,0:T(8,128)(2,1)}), bf16[16,40,512]{2,1,0:T(8,128)(2,1)}, u32[]{:S(2)}, u32[]{:S(2)}) async-start(bf16[16,40,512]{2,1,0:T(8,128)(2,1)} %get-tuple-element.8), calls=%async_computation.2 | async-start | bytes 1310720 | tf_op jit(solution)/shard_map/all_to_all | solution.py:243
  124.7 0.9 copy-start.4

commit v3 on v2

--- a/solution.py
+++ b/solution.py
@@ -7,6 +7,8 @@
 from jax.experimental.pallas import tpu as pltpu
 from jax.sharding import PartitionSpec as P
 
+AXES = ("segment", "dp", "expert")
+LOW = 4
 PIECES = 4
 F32 = jnp.float32
 BF16 = jnp.bfloat16
@@ -18,6 +20,23 @@
     return lax.ppermute(value, axis, pairs)
 
 
+def token_groups():
+    sections, parts, experts = (lax.axis_size(axis) for axis in AXES)
+    line = parts * LOW
+    groups = []
+    for section in range(sections):
+        shift = LOW // 2 if section % 2 else 0
+        for part in range(parts):
+            where = {}
+            for step in range(LOW):
+                spot = (part * LOW + shift + step) % line
+                for far in range(experts // LOW):
+                    expert = far * LOW + spot % LOW
+                    where[expert] = (section * parts + spot // LOW) * experts + expert
+            groups.append([where[expert] for expert in range(experts)])
+    return groups
+
+
 def silu_grad(value):
     sigma = jax.nn.sigmoid(value)
     return sigma * (1.0 + value * (1.0 - sigma))
@@ -43,15 +62,20 @@
 
 
 def slots_along_lanes(route, experts):
-    tokens = route.shape[0]
+    tokens = route.shape[1]
     square = (tokens, tokens)
-    lane_route = jnp.sum(
-        jnp.where(iota(square, 0) == iota(square, 1), route.astype(F32), 0.0), axis=0, keepdims=True
-    )
+    lane_route = route.astype(F32)
     named = one_hot(iota((experts, tokens), 0).astype(F32) == lane_route)
     before = dot(named, one_hot(iota(square, 0) < iota(square, 1)))
     rank = jnp.sum(before * named.astype(F32), axis=0, keepdims=True)
     return lane_route.astype(jnp.int32), rank.astype(jnp.int32)
+
+
+def upright(row):
+    square = (row.shape[1], row.shape[1])
+    return jnp.sum(
+        jnp.where(iota(square, 0) == iota(square, 1), row.astype(F32), 0.0), axis=1, keepdims=True
+    )
 
 
 def slots_along_sublanes(route):
@@ -79,19 +103,27 @@
 
 
 def dispatch_g_kernel(capacity, experts, route_ref, gate_ref, values_ref, out_ref):
-    scaled = (gate_ref[...] * values_ref[...].astype(F32)).astype(BF16)
+    scaled = (upright(gate_ref[...]) * values_ref[...].astype(F32)).astype(BF16)
     out_ref[...] = place(route_ref[...], scaled, capacity, experts, out_ref.shape[0])
 
 
-def combine_kernel(capacity, route_ref, rows_ref, _after_ref, out_ref):
-    route = route_ref[...]
+def combine_kernel(capacity, route_ref, rows_hbm, _after_ref, out_hbm, rows_ref, out_ref, sem, sems):
+    fetch = pltpu.make_async_copy(rows_hbm, rows_ref, sem)
+    fetch.start()
+    route = upright(route_ref[...]).astype(jnp.int32)
     rank = slots_along_sublanes(route)
-    rows = rows_ref[...]
-    count, short = rows.shape
+    count, short = rows_ref.shape
     at = iota((route.shape[0], count), 1)
-    for p in range(PIECES):
-        table = one_hot(at == first_short_row(route, rank, capacity, p))
-        out_ref[:, p * short : (p + 1) * short] = dot(table, rows).astype(BF16)
+    tables = [one_hot(at == first_short_row(route, rank, capacity, p)) for p in range(PIECES)]
+    fetch.wait()
+    copies = []
+    for p, table in enumerate(tables):
+        here = pl.ds(p * short, short)
+        out_ref[:, p * short : (p + 1) * short] = dot(table, rows_ref[...]).astype(BF16)
+        copies.append(pltpu.make_async_copy(out_ref.at[:, here], out_hbm.at[:, here], sems.at[p]))
+        copies[-1].start()
+    for copy in copies:
+        copy.wait()
 
 
 def rest_table(chunks, rest, piece, dim):
@@ -224,6 +256,7 @@
         out_specs=(out_spec,) * len(outs) if many else out_spec,
         scratch_shapes=list(scratch),
         compiler_params=pltpu.CompilerParams(vmem_limit_bytes=24 * 2**20),
+        name=getattr(kernel, "func", kernel).__name__.split("_")[0],
         cost_estimate=pl.CostEstimate(flops=flops, bytes_accessed=moved, transcendentals=0),
     )(*args)
 
@@ -237,15 +270,18 @@
     chunk, short = PIECES * capacity, width // PIECES
     count = experts * chunk
     table = jax.ShapeDtypeStruct((count, short), BF16)
-    route, weight_in, weight_out = route_b[0], w_in[0, 0], w_out[0, 0]
+    route, gate = route_b.reshape(1, tokens), gate_b.reshape(1, tokens)
+    weight_in, weight_out = w_in[0, 0], w_out[0, 0]
 
     def exchange(rows):
-        return lax.all_to_all(rows, "expert", split_axis=0, concat_axis=0, tiled=True)
+        return lax.all_to_all(
+            rows, AXES, split_axis=0, concat_axis=0, tiled=True, axis_index_groups=token_groups()
+        )
 
     arrived = passed_along(grad_y_b, "segment", -1)[0]
     send_x = call(functools.partial(dispatch_x_kernel, capacity, experts), table, (route, saved_b[0]))
     recv_x = exchange(send_x.reshape(experts, chunk, short))
-    send_g = call(functools.partial(dispatch_g_kernel, capacity, experts), table, (route, gate_b[0], arrived))
+    send_g = call(functools.partial(dispatch_g_kernel, capacity, experts), table, (route, gate, arrived))
     recv_g = exchange(send_g.reshape(experts, chunk, short))
     x_from_below = passed_along(recv_x, "dp", 1)
     x_from_above = passed_along(recv_x, "dp", -1)
@@ -253,7 +289,7 @@
         functools.partial(pre_kernel, capacity),
         pltpu.HBM((experts * capacity, hidden), F32),
         (recv_x, weight_in),
-        flops=1000,
+        flops=2*10**13,
         moved=1000,
     )
     columns = pltpu.HBM((experts * capacity, hidden // parts), BF16)
@@ -274,7 +310,7 @@
             pltpu.SemaphoreType.DMA((4 + PIECES,)),
             pltpu.SemaphoreType.DMA((2 + 2 * PIECES,)),
         ],
-        flops=1000,
+        flops=5*10**12,
         moved=1000,
     )
     home = exchange(back)
@@ -288,8 +324,16 @@
     )
     grad_x = call(
         functools.partial(combine_kernel, capacity),
-        jax.ShapeDtypeStruct((tokens, width), BF16),
-        (route, home.reshape(count, short), done),
+        pltpu.HBM((tokens, width), BF16),
+        (route, in_hbm(home.reshape(count, short)), done),
+        specs=[VMEM, ANY, VMEM],
+        out_spec=ANY,
+        scratch=[
+            pltpu.VMEM((count, short), BF16),
+            pltpu.VMEM((tokens, width), BF16),
+            pltpu.SemaphoreType.DMA(()),
+            pltpu.SemaphoreType.DMA((PIECES,)),
+        ],
         flops=1000,
         moved=1000,
     )

time: 145 us -> 136 us (0.938)
  starting transfers between devices: 52.2 us -> 44.5 us
  local copies, waits for them, and re-layouts: 4.49 us -> 2.64 us
    all_to_all x3, waiting for transfers between devices: 60.3 us -> 45.7 us  [exchange(): lax.all_to_all(rows, AXES, split_axis=0, concat_axis=0, tiled=True, axis_...]
    ppermute x5, starting transfers between devices: 32.6 us -> 18.4 us  [passed_along(): return lax.ppermute(value, axis, pairs)]
    ppermute x5, waiting for transfers between devices: 8.39 us -> 22.4 us  [passed_along(): return lax.ppermute(value, axis, pairs)]
    all_to_all x3, starting transfers between devices: 19.6 us -> 26.1 us  [exchange(): lax.all_to_all(rows, AXES, split_axis=0, concat_axis=0, tiled=True, axis_...]
    unnamed x12 -> x14, local copies, waits for them, and re-layouts: 3.61 us -> 2.64 us
  transfers between devices with their start and end apart: 8 -> 8, of which waited for: 5 -> 5; matrix products, arithmetic and copies ran while one was open for 0% -> 0% of each run, Pallas kernels for 10% -> 11%
where the time goes in v3:
time: 136 us; the launch traced here: 135 us
  waiting for transfers between devices  68.1 us (50%)
  starting transfers between devices  44.5 us (33%)
  Pallas kernels  19.1 us (14%)
  local copies, waits for them, and re-layouts  2.64 us (2%)
    all_to_all x3, waiting for transfers between devices, exchange(): lax.all_to_all(rows, AXES, split_axis=0, concat_axis=0, tiled=True, axis_...  45.7 us
    all_to_all x3, starting transfers between devices, exchange(): lax.all_to_all(rows, AXES, split_axis=0, concat_axis=0, tiled=True, axis_...  26.1 us
    ppermute x5, waiting for transfers between devices, passed_along(): return lax.ppermute(value, axis, pairs)  22.4 us
    pallas_call x6, Pallas kernels, call(): pl.pallas_call(kernel, out_shape=outs, in_specs=specs or [VMEM] * len(arg...  19.1 us
    ppermute x5, starting transfers between devices, passed_along(): return lax.ppermute(value, axis, pairs)  18.4 us
  transfers between devices with their start and end apart: 8, of which 5 were waited for; matrix products, arithmetic and copies ran while one was open for 0% of the time, Pallas kernels for 11%

profile of v3, /device:TPU:1, one launch (start us, length us, event | category | flops | bytes accessed | tf_op | source)
XLA Modules:
  0.0 135.1 jit_solution(15836400743941951865)
XLA Ops:
  0.6 0.0 copy-start.1
  0.6 0.0 copy-start.5
  0.7 0.0 copy-start
  0.7 0.7 copy-done
  1.4 1.0 copy-done.4
  2.4 1.5 %dispatch.3 = bf16[640,512]{1,0:T(8,128)(2,1)} custom-call(s32[1,128]{1,0:T(1,128)S(1)} %bitcast.12, bf16[128,2048]{1,0:T(8,128)(2,1)S(1)} %bitcast.17), custom_call_target="tpu_custom_call" | custom-call | flops 1000000000 | bytes 4000000 | tf_op jit(solution)/shard_map/dispatch/pallas_call | solution.py:252
  3.9 17.4 %all-to-all-start.1 = ((bf16[16,40,512]{2,1,0:T(8,128)(2,1)}), bf16[16,40,512]{2,1,0:T(8,128)(2,1)}, u32[]{:S(2)}, u32[]{:S(2)}) async-start(bf16[16,40,512]{2,1,0:T(8,128)(2,1)} %bitcast.6), calls=%async_computation.1 | async-start | bytes 1310720 | tf_op jit(solution)/shard_map/all_to_all | solution.py:277
  21.3 0.0 collective-permute-start
  21.4 9.2 %collective-permute-done = bf16[1,128,2048]{2,1,0:T(8,128)(2,1)} collective-permute-done((bf16[1,128,2048]{2,1,0:T(8,128)(2,1)}, bf16[1,128,2048]{2,1,0:T(8,128)(2,1)}, u32[]{:S(2)}, u32[]{:S(2)}) %collective-permute-start) | collective-permute-done | bytes 524320 | tf_op jit(solution)/shard_map/ppermute | solution.py:20
  30.6 0.0 copy-done.1
  30.6 0.0 copy-done.5
  30.6 2.6 %dispatch.2 = bf16[640,512]{1,0:T(8,128)(2,1)} custom-call(s32[1,128]{1,0:T(1,128)S(1)} %bitcast.13, f32[1,128]{1,0:T(1,128)S(1)} %bitcast.18, bf16[128,2048]{1,0:T(8,128)(2,1)} %bitcast.3.values_ref), custom_call_target="tpu_custom_call" | custom-call | flops 1000000000 | bytes 4000000 | tf_op jit(solution)/shard_map/dispatch/pallas_call | solution.py:252
  33.1 5.6 %all-to-all-done.1.rows_ref.refs_0_ = bf16[16,40,512]{2,1,0:T(8,128)(2,1)} async-done(((bf16[16,40,512]{2,1,0:T(8,128)(2,1)}), bf16[16,40,512]{2,1,0:T(8,128)(2,1)}, u32[]{:S(2)}, u32[]{:S(2)}) %all-to-all-start.1) | async-done | bytes 655392 | tf_op jit(solution)/shard_map/all_to_all | solution.py:277
  38.7 4.3 %all-to-all-start = ((bf16[16,40,512]{2,1,0:T(8,128)(2,1)}), bf16[16,40,512]{2,1,0:T(8,128)(2,1)}, u32[]{:S(2)}, u32[]{:S(2)}) async-start(bf16[16,40,512]{2,1,0:T(8,128)(2,1)} %bitcast.4), calls=%async_computation | async-start | bytes 1310720 | tf_op jit(solution)/shard_map/all_to_all | solution.py:277
  43.0 3.4 %collective-permute-start.2 = (bf16[16,40,512]{2,1,0:T(8,128)(2,1)}, bf16[16,40,512]{2,1,0:T(8,128)(2,1)}, u32[]{:S(2)}, u32[]{:S(2)}) collective-permute-start(bf16[16,40,512]{2,1,0:T(8,128)(2,1)} %all-to-all-done.1.rows_ref.refs_0_), channel_id=1, source_target_pairs={{0,32},{16,0},{32,16},{1,33},{17,1},{33,17},{2,34},{18,2},{34,18},... | collective-permute-start | bytes 1966088 | tf_op jit(solution)/shard_map/ppermute | solution.py:20
  46.4 5.8 %collective-permute-start.1 = (bf16[16,40,512]{2,1,0:T(8,128)(2,1)}, bf16[16,40,512]{2,1,0:T(8,128)(2,1)}, u32[]{:S(2)}, u32[]{:S(2)}) collective-permute-start(bf16[16,40,512]{2,1,0:T(8,128)(2,1)} %all-to-all-done.1.rows_ref.refs_0_), channel_id=1, source_target_pairs={{0,16},{16,32},{32,0},{1,17},{17,33},{33,1},{2,18},{18,34},{34,2},... | collective-permute-start | bytes 1966088 | tf_op jit(solution)/shard_map/ppermute | solution.py:20
  52.2 0.0 copy-done.3
  52.2 2.8 %pre.1.pre_hbm = f32[160,768]{1,0:T(8,128)} custom-call(bf16[16,40,512]{2,1,0:T(8,128)(2,1)} %all-to-all-done.1.rows_ref.refs_0_, bf16[2048,768]{1,0:T(8,128)(2,1)S(1)} %bitcast.16), custom_call_target="tpu_custom_call" | custom-call | flops 19999999655936 | bytes 1000 | tf_op jit(solution)/shard_map/pre/pallas_call | solution.py:252
  55.0 33.8 %all-to-all-done.rows_hbm = bf16[16,40,512]{2,1,0:T(8,128)(2,1)} async-done(((bf16[16,40,512]{2,1,0:T(8,128)(2,1)}), bf16[16,40,512]{2,1,0:T(8,128)(2,1)}, u32[]{:S(2)}, u32[]{:S(2)}) %all-to-all-start) | async-done | bytes 655392 | tf_op jit(solution)/shard_map/all_to_all | solution.py:277
  88.8 6.2 %expert.1 = (bf16[16,40,512]{2,1,0:T(8,128)(2,1)}, bf16[160,256]{1,0:T(8,128)(2,1)}, bf16[160,256]{1,0:T(8,128)(2,1)}, bf16[160,256]{1,0:T(8,128)(2,1)}) custom-call(s32[1]{0:T(128)} %bitcast.1.place_ref, bf16[16,40,512]{2,1,0:T(8,128)(2,1)} %all-to-all-done.rows_hbm, f32[160,768]{1,0:T(8,128)} %pre.1.pre_hbm, bf16[2048,768]{1,0:T(8,128)(2,1)} %bitcast.15, ...), custom_call_target="tpu_custom_call" | custom-call | flops 4999999913984 | bytes 1000 | tf_op jit(solution)/shard_map/expert/pallas_call | solution.py:252
  95.1 1.9 %collective-permute-start.3 = (bf16[160,256]{1,0:T(8,128)(2,1)}, bf16[160,256]{1,0:T(8,128)(2,1)S(1)}, u32[]{:S(2)}, u32[]{:S(2)}) collective-permute-start(bf16[160,256]{1,0:T(8,128)(2,1)} %get-tuple-element.10), channel_id=1, source_target_pairs={{0,16},{16,32},{32,0},{1,17},{17,33},{33,1},{2,18},{18,34},{34,2},... | collective-permute-start | bytes 245768 | tf_op jit(solution)/shard_map/ppermute | solution.py:20
  97.0 7.3 %collective-permute-start.4 = (bf16[160,256]{1,0:T(8,128)(2,1)}, bf16[160,256]{1,0:T(8,128)(2,1)S(1)}, u32[]{:S(2)}, u32[]{:S(2)}) collective-permute-start(bf16[160,256]{1,0:T(8,128)(2,1)} %get-tuple-element.11), channel_id=1, source_target_pairs={{0,32},{16,0},{32,16},{1,33},{17,1},{33,17},{2,34},{18,2},{34,18},... | collective-permute-start | bytes 245768 | tf_op jit(solution)/shard_map/ppermute | solution.py:20
  104.3 4.5 %all-to-all-start.2 = ((bf16[16,40,512]{2,1,0:T(8,128)(2,1)}), bf16[16,40,512]{2,1,0:T(8,128)(2,1)}, u32[]{:S(2)}, u32[]{:S(2)}) async-start(bf16[16,40,512]{2,1,0:T(8,128)(2,1)} %get-tuple-element.8), calls=%async_computation.2 | async-start | bytes 1310720 | tf_op jit(solution)/shard_map/all_to_all | solution.py:277
  108.7 13.2 %collective-permute-done.3.refs_4_ = bf16[160,256]{1,0:T(8,128)(2,1)S(1)} collective-permute-done((bf16[160,256]{1,0:T(8,128)(2,1)}, bf16[160,256]{1,0:T(8,128)(2,1)S(1)}, u32[]{:S(2)}, u32[]{:S(2)}) %collective-permute-start.3) | collective-permute-done | bytes 81952 | tf_op jit(solution)/shard_map/ppermute | solution.py:20
  121.9 0.0 collective-permute-done.4.refs_5_
  121.9 0.0 collective-permute-done.2.refs_2_
  121.9 0.0 collective-permute-done.1.refs_1_
  121.9 0.0 copy-start.6
  121.9 0.9 copy-done.6
  122.8 3.6 %weight.1 = (bf16[2048,256]{1,0:T(8,128)(2,1)}, f32[8,128]{1,0:T(8,128)S(1)}) custom-call(bf16[16,40,512]{2,1,0:T(8,128)(2,1)} %all-to-all-done.1.rows_ref.refs_0_, bf16[16,40,512]{2,1,0:T(8,128)(2,1)} %collective-permute-done.1.refs_1_, bf16[16,40,512]{2,1,0:T(8,128)(2,1)} %collective-permute-done.2.refs_2_, bf16[160,256]{1,0:T(8,128)(2,1)S(1)} %copy-done.6, ...), custom_call_target="tpu_custom_call" | custom-call | flops 4999999913984 | bytes 4000000 | tf_op jit(solution)/shard_map/weight/pallas_call | solution.py:252
  126.4 6.3 %all-to-all-done.2 = bf16[16,40,512]{2,1,0:T(8,128)(2,1)} async-done(((bf16[16,40,512]{2,1,0:T(8,128)(2,1)}), bf16[16,40,512]{2,1,0:T(8,128)(2,1)}, u32[]{:S(2)}, u32[]{:S(2)}) %all-to-all-start.2) | async-done | bytes 655392 | tf_op jit(solution)/shard_map/all_to_all | solution.py:277
  132.7 2.4 %combine.1 = bf16[128,2048]{1,0:T(8,128)(2,1)} custom-call(s32[1,128]{1,0:T(1,128)S(1)} %bitcast.14, bf16[640,512]{1,0:T(8,128)(2,1)} %bitcast.9.rows_hbm, f32[8,128]{1,0:T(8,128)S(1)} %get-tuple-element.12._after_ref), custom_call_target="tpu_custom_call" | custom-call | flops 1000 | bytes 1000 | tf_op jit(solution)/shard_map/combine/pallas_call | solution.py:252
  (4 shorter events, 0.0 us)
Async XLA Ops:
  0.6 29.9 %copy-start.1 = (s32[1,128,1]{1,2,0:T(1,128)S(1)}, s32[1,128,1]{1,2,0:T(1,128)}, u32[]{:S(2)}) copy-start(s32[1,128,1]{1,2,0:T(1,128)} %param.7) | copy-start | bytes 1540
  0.6 29.9 %copy-start.5 = (f32[1,128,1]{1,2,0:T(1,128)S(1)}, f32[1,128,1]{1,2,0:T(1,128)}, u32[]{:S(2)}) copy-start(f32[1,128,1]{1,2,0:T(1,128)} %param.8) | copy-start | bytes 1540
  0.7 0.7 copy-start
  1.4 1.0 copy-start.4
  3.9 48.2 %copy-start.3 = (bf16[1,1,2048,768]{3,2,1,0:T(8,128)(2,1)S(1)}, bf16[1,1,2048,768]{3,2,1,0:T(8,128)(2,1)}, u32[]{:S(2)}) copy-start(bf16[1,1,2048,768]{3,2,1,0:T(8,128)(2,1)} %param.10) | copy-start | bytes 9437188
  3.9 34.8 %all-to-all-start.1 = ((bf16[16,40,512]{2,1,0:T(8,128)(2,1)}), bf16[16,40,512]{2,1,0:T(8,128)(2,1)}, u32[]{:S(2)}, u32[]{:S(2)}) async-start(bf16[16,40,512]{2,1,0:T(8,128)(2,1)} %bitcast.6), calls=%async_computation.1 | async-start | bytes 1310720 | tf_op jit(solution)/shard_map/all_to_all | solution.py:277
  21.3 9.2 %collective-permute-start = (bf16[1,128,2048]{2,1,0:T(8,128)(2,1)}, bf16[1,128,2048]{2,1,0:T(8,128)(2,1)}, u32[]{:S(2)}, u32[]{:S(2)}) collective-permute-start(bf16[1,128,2048]{2,1,0:T(8,128)(2,1)} %param.9), channel_id=1, source_target_pairs={{0,720},{48,0},{96,48},{144,96},{192,144},{240,192},{288,240},{336... | collective-permute-start | bytes 1572872 | tf_op jit(solution)/shard_map/ppermute | solution.py:20
  38.7 50.1 %all-to-all-start = ((bf16[16,40,512]{2,1,0:T(8,128)(2,1)}), bf16[16,40,512]{2,1,0:T(8,128)(2,1)}, u32[]{:S(2)}, u32[]{:S(2)}) async-start(bf16[16,40,512]{2,1,0:T(8,128)(2,1)} %bitcast.4), calls=%async_computation | async-start | bytes 1310720 | tf_op jit(solution)/shard_map/all_to_all | solution.py:277
  43.0 78.9 %collective-permute-start.2 = (bf16[16,40,512]{2,1,0:T(8,128)(2,1)}, bf16[16,40,512]{2,1,0:T(8,128)(2,1)}, u32[]{:S(2)}, u32[]{:S(2)}) collective-permute-start(bf16[16,40,512]{2,1,0:T(8,128)(2,1)} %all-to-all-done.1.rows_ref.refs_0_), channel_id=1, source_target_pairs={{0,32},{16,0},{32,16},{1,33},{17,1},{33,17},{2,34},{18,2},{34,18},... | collective-permute-start | bytes 1966088 | tf_op jit(solution)/shard_map/ppermute | solution.py:20
  46.4 75.6 %collective-permute-start.1 = (bf16[16,40,512]{2,1,0:T(8,128)(2,1)}, bf16[16,40,512]{2,1,0:T(8,128)(2,1)}, u32[]{:S(2)}, u32[]{:S(2)}) collective-permute-start(bf16[16,40,512]{2,1,0:T(8,128)(2,1)} %all-to-all-done.1.rows_ref.refs_0_), channel_id=1, source_target_pairs={{0,16},{16,32},{32,0},{1,17},{17,33},{33,1},{2,18},{18,34},{34,2},... | collective-permute-start | bytes 1966088 | tf_op jit(solution)/shard_map/ppermute | solution.py:20
  95.1 26.9 %collective-permute-start.3 = (bf16[160,256]{1,0:T(8,128)(2,1)}, bf16[160,256]{1,0:T(8,128)(2,1)S(1)}, u32[]{:S(2)}, u32[]{:S(2)}) collective-permute-start(bf16[160,256]{1,0:T(8,128)(2,1)} %get-tuple-element.10), channel_id=1, source_target_pairs={{0,16},{16,32},{32,0},{1,17},{17,33},{33,1},{2,18},{18,34},{34,2},... | collective-permute-start | bytes 245768 | tf_op jit(solution)/shard_map/ppermute | solution.py:20
  97.0 24.9 %collective-permute-start.4 = (bf16[160,256]{1,0:T(8,128)(2,1)}, bf16[160,256]{1,0:T(8,128)(2,1)S(1)}, u32[]{:S(2)}, u32[]{:S(2)}) collective-permute-start(bf16[160,256]{1,0:T(8,128)(2,1)} %get-tuple-element.11), channel_id=1, source_target_pairs={{0,32},{16,0},{32,16},{1,33},{17,1},{33,17},{2,34},{18,2},{34,18},... | collective-permute-start | bytes 245768 | tf_op jit(solution)/shard_map/ppermute | solution.py:20
  104.3 28.5 %all-to-all-start.2 = ((bf16[16,40,512]{2,1,0:T(8,128)(2,1)}), bf16[16,40,512]{2,1,0:T(8,128)(2,1)}, u32[]{:S(2)}, u32[]{:S(2)}) async-start(bf16[16,40,512]{2,1,0:T(8,128)(2,1)} %get-tuple-element.8), calls=%async_computation.2 | async-start | bytes 1310720 | tf_op jit(solution)/shard_map/all_to_all | solution.py:277
  121.9 0.9 copy-start.6
  122.8 9.9 %copy-start.2 = (s32[1,128,1]{1,2,0:T(1,128)S(1)}, s32[1,128,1]{1,2,0:T(1,128)}, u32[]{:S(2)}) copy-start(s32[1,128,1]{1,2,0:T(1,128)} %param.7) | copy-start | bytes 1540

commit v4 on v3

--- a/solution.py
+++ b/solution.py
@@ -86,25 +86,42 @@
     return jnp.sum(before * named.astype(F32), axis=1, keepdims=True).astype(jnp.int32)
 
 
-def place(route, values, capacity, experts, rows):
-    tokens, width = values.shape
+def dispatch_kernel(capacity, experts, refs, scale):
+    route_hbm, values_hbm, out_hbm, route_ref, values_ref, out_ref, sems = refs
+    fetch_route = pltpu.make_async_copy(route_hbm, route_ref, sems.at[0])
+    fetch_route.start()
+    fetch_values = pltpu.make_async_copy(values_hbm, values_ref, sems.at[1])
+    fetch_values.start()
+    fetch_route.wait()
+    rows = out_ref.shape[0]
+    tokens, width = values_ref.shape
     short = width // PIECES
-    lane_route, rank = slots_along_lanes(route, experts)
+    lane_route, rank = slots_along_lanes(route_ref[...], experts)
     at = iota((rows, tokens), 0)
     table = jnp.concatenate(
         [one_hot(at == first_short_row(lane_route, rank, capacity, p)) for p in range(PIECES)], axis=1
     )
+    fetch_values.wait()
+    values = scale(values_ref[...])
     stacked = jnp.concatenate([values[:, p * short : (p + 1) * short] for p in range(PIECES)], axis=0)
-    return dot(table, stacked).astype(BF16)
-
-
-def dispatch_x_kernel(capacity, experts, route_ref, values_ref, out_ref):
-    out_ref[...] = place(route_ref[...], values_ref[...], capacity, experts, out_ref.shape[0])
-
-
-def dispatch_g_kernel(capacity, experts, route_ref, gate_ref, values_ref, out_ref):
-    scaled = (upright(gate_ref[...]) * values_ref[...].astype(F32)).astype(BF16)
-    out_ref[...] = place(route_ref[...], scaled, capacity, experts, out_ref.shape[0])
+    copies = []
+    half = rows // 2
+    for i in range(2):
+        here = pl.ds(i * half, half)
+        out_ref[here, :] = dot(table[i * half : (i + 1) * half], stacked).astype(BF16)
+        copies.append(pltpu.make_async_copy(out_ref.at[here, :], out_hbm.at[here, :], sems.at[2 + i]))
+        copies[-1].start()
+    for copy in copies:
+        copy.wait()
+
+
+def dispatch_x_kernel(capacity, experts, *refs):
+    dispatch_kernel(capacity, experts, refs, lambda values: values)
+
+
+def dispatch_g_kernel(capacity, experts, gate_ref, *refs):
+    gate = upright(gate_ref[...])
+    dispatch_kernel(capacity, experts, refs, lambda values: (gate * values.astype(F32)).astype(BF16))
 
 
 def combine_kernel(capacity, route_ref, rows_hbm, _after_ref, out_hbm, rows_ref, out_ref, sem, sems):
@@ -269,7 +286,7 @@
     capacity = max(2, tokens * 5 // (4 * experts))
     chunk, short = PIECES * capacity, width // PIECES
     count = experts * chunk
-    table = jax.ShapeDtypeStruct((count, short), BF16)
+    table = pltpu.HBM((count, short), BF16)
     route, gate = route_b.reshape(1, tokens), gate_b.reshape(1, tokens)
     weight_in, weight_out = w_in[0, 0], w_out[0, 0]
 
@@ -279,9 +296,30 @@
         )
 
     arrived = passed_along(grad_y_b, "segment", -1)[0]
-    send_x = call(functools.partial(dispatch_x_kernel, capacity, experts), table, (route, saved_b[0]))
+    scratch = [
+        pltpu.VMEM((1, tokens), jnp.int32),
+        pltpu.VMEM((tokens, width), BF16),
+        pltpu.VMEM((count, short), BF16),
+        pltpu.SemaphoreType.DMA((4,)),
+    ]
+    send_x = call(
+        functools.partial(dispatch_x_kernel, capacity, experts),
+        table,
+        (in_hbm(route), in_hbm(saved_b[0])),
+        specs=[ANY, ANY],
+        out_spec=ANY,
+        scratch=scratch,
+    )
     recv_x = exchange(send_x.reshape(experts, chunk, short))
-    send_g = call(functools.partial(dispatch_g_kernel, capacity, experts), table, (route, gate, arrived))
+    send_g = call(
+        functools.partial(dispatch_g_kernel, capacity, experts),
+        table,
+        (gate, in_hbm(route), in_hbm(arrived)),
+        specs=[VMEM, ANY, ANY],
+        out_spec=ANY,
+        scratch=scratch,
+        flops=10**9,
+    )
     recv_g = exchange(send_g.reshape(experts, chunk, short))
     x_from_below = passed_along(recv_x, "dp", 1)
     x_from_above = passed_along(recv_x, "dp", -1)

time: 136 us -> 135 us (level)
  local copies, waits for them, and re-layouts: 2.64 us -> 0.9 us
    unnamed x14 -> x8, local copies, waits for them, and re-layouts: 2.64 us -> 0.9 us
where the time goes in v4:
time: 135 us; the launch traced here: 134 us
  waiting for transfers between devices  68.5 us (51%)
  starting transfers between devices  44.6 us (33%)
  Pallas kernels  19.7 us (15%)
    all_to_all x3, waiting for transfers between devices, exchange(): lax.all_to_all(rows, AXES, split_axis=0, concat_axis=0, tiled=True, axis_...  46.2 us
    all_to_all x3, starting transfers between devices, exchange(): lax.all_to_all(rows, AXES, split_axis=0, concat_axis=0, tiled=True, axis_...  26.2 us
    ppermute x5, waiting for transfers between devices, passed_along(): return lax.ppermute(value, axis, pairs)  22.3 us
    pallas_call x6, Pallas kernels, call(): pl.pallas_call(kernel, out_shape=outs, in_specs=specs or [VMEM] * len(arg...  19.7 us
    ppermute x5, starting transfers between devices, passed_along(): return lax.ppermute(value, axis, pairs)  18.4 us
  transfers between devices with their start and end apart: 8, of which 5 were waited for; matrix products, arithmetic and copies ran while one was open for 0% of the time, Pallas kernels for 11%

profile of v4, /device:TPU:1, one launch (start us, length us, event | category | flops | bytes accessed | tf_op | source)
XLA Modules:
  0.0 134.4 jit_solution(4444077785952696863)
XLA Ops:
  0.6 0.0 copy-start.2
  0.6 2.4 %dispatch.3 = bf16[640,512]{1,0:T(8,128)(2,1)} custom-call(s32[1,128]{1,0:T(1,128)} %bitcast.12, bf16[128,2048]{1,0:T(8,128)(2,1)} %bitcast.22), custom_call_target="tpu_custom_call" | custom-call | flops 1000000000 | bytes 4000000 | tf_op jit(solution)/shard_map/dispatch/pallas_call | solution.py:269
  3.0 0.0 copy-start.1
  3.0 17.4 %all-to-all-start.1 = ((bf16[16,40,512]{2,1,0:T(8,128)(2,1)}), bf16[16,40,512]{2,1,0:T(8,128)(2,1)}, u32[]{:S(2)}, u32[]{:S(2)}) async-start(bf16[16,40,512]{2,1,0:T(8,128)(2,1)} %bitcast.18), calls=%async_computation.1 | async-start | bytes 1310720 | tf_op jit(solution)/shard_map/all_to_all | solution.py:294
  20.4 0.0 collective-permute-start
  20.5 9.2 %collective-permute-done = bf16[1,128,2048]{2,1,0:T(8,128)(2,1)} collective-permute-done((bf16[1,128,2048]{2,1,0:T(8,128)(2,1)}, bf16[1,128,2048]{2,1,0:T(8,128)(2,1)}, u32[]{:S(2)}, u32[]{:S(2)}) %collective-permute-start) | collective-permute-done | bytes 524320 | tf_op jit(solution)/shard_map/ppermute | solution.py:20
  29.6 0.0 copy-done.2
  29.6 2.3 %dispatch.2 = bf16[640,512]{1,0:T(8,128)(2,1)} custom-call(f32[1,128]{1,0:T(1,128)S(1)} %bitcast.17, s32[1,128]{1,0:T(1,128)} %bitcast.13, bf16[128,2048]{1,0:T(8,128)(2,1)} %bitcast.3.refs_1_), custom_call_target="tpu_custom_call" | custom-call | flops 1000000000 | bytes 4000000 | tf_op jit(solution)/shard_map/dispatch/pallas_call | solution.py:269
  32.0 5.8 %all-to-all-done.1.rows_ref.refs_0_ = bf16[16,40,512]{2,1,0:T(8,128)(2,1)} async-done(((bf16[16,40,512]{2,1,0:T(8,128)(2,1)}), bf16[16,40,512]{2,1,0:T(8,128)(2,1)}, u32[]{:S(2)}, u32[]{:S(2)}) %all-to-all-start.1) | async-done | bytes 655392 | tf_op jit(solution)/shard_map/all_to_all | solution.py:294
  37.8 4.3 %all-to-all-start = ((bf16[16,40,512]{2,1,0:T(8,128)(2,1)}), bf16[16,40,512]{2,1,0:T(8,128)(2,1)}, u32[]{:S(2)}, u32[]{:S(2)}) async-start(bf16[16,40,512]{2,1,0:T(8,128)(2,1)} %bitcast.19), calls=%async_computation | async-start | bytes 1310720 | tf_op jit(solution)/shard_map/all_to_all | solution.py:294
  42.1 3.4 %collective-permute-start.2 = (bf16[16,40,512]{2,1,0:T(8,128)(2,1)}, bf16[16,40,512]{2,1,0:T(8,128)(2,1)}, u32[]{:S(2)}, u32[]{:S(2)}) collective-permute-start(bf16[16,40,512]{2,1,0:T(8,128)(2,1)} %all-to-all-done.1.rows_ref.refs_0_), channel_id=1, source_target_pairs={{0,32},{16,0},{32,16},{1,33},{17,1},{33,17},{2,34},{18,2},{34,18},... | collective-permute-start | bytes 1966088 | tf_op jit(solution)/shard_map/ppermute | solution.py:20
  45.4 5.8 %collective-permute-start.1 = (bf16[16,40,512]{2,1,0:T(8,128)(2,1)}, bf16[16,40,512]{2,1,0:T(8,128)(2,1)}, u32[]{:S(2)}, u32[]{:S(2)}) collective-permute-start(bf16[16,40,512]{2,1,0:T(8,128)(2,1)} %all-to-all-done.1.rows_ref.refs_0_), channel_id=1, source_target_pairs={{0,16},{16,32},{32,0},{1,17},{17,33},{33,1},{2,18},{18,34},{34,2},... | collective-permute-start | bytes 1966088 | tf_op jit(solution)/shard_map/ppermute | solution.py:20
  51.3 0.0 copy-done.1
  51.3 2.8 %pre.1.pre_hbm = f32[160,768]{1,0:T(8,128)} custom-call(bf16[16,40,512]{2,1,0:T(8,128)(2,1)} %all-to-all-done.1.rows_ref.refs_0_, bf16[2048,768]{1,0:T(8,128)(2,1)S(1)} %bitcast.16), custom_call_target="tpu_custom_call" | custom-call | flops 19999999655936 | bytes 1000 | tf_op jit(solution)/shard_map/pre/pallas_call | solution.py:269
  54.1 33.7 %all-to-all-done.rows_hbm = bf16[16,40,512]{2,1,0:T(8,128)(2,1)} async-done(((bf16[16,40,512]{2,1,0:T(8,128)(2,1)}), bf16[16,40,512]{2,1,0:T(8,128)(2,1)}, u32[]{:S(2)}, u32[]{:S(2)}) %all-to-all-start) | async-done | bytes 655392 | tf_op jit(solution)/shard_map/all_to_all | solution.py:294
  87.8 6.2 %expert.1 = (bf16[16,40,512]{2,1,0:T(8,128)(2,1)}, bf16[160,256]{1,0:T(8,128)(2,1)}, bf16[160,256]{1,0:T(8,128)(2,1)}, bf16[160,256]{1,0:T(8,128)(2,1)}) custom-call(s32[1]{0:T(128)} %bitcast.1.place_ref, bf16[16,40,512]{2,1,0:T(8,128)(2,1)} %all-to-all-done.rows_hbm, f32[160,768]{1,0:T(8,128)} %pre.1.pre_hbm, bf16[2048,768]{1,0:T(8,128)(2,1)} %bitcast.15, ...), custom_call_target="tpu_custom_call" | custom-call | flops 4999999913984 | bytes 1000 | tf_op jit(solution)/shard_map/expert/pallas_call | solution.py:269
  94.0 1.9 %collective-permute-start.3 = (bf16[160,256]{1,0:T(8,128)(2,1)}, bf16[160,256]{1,0:T(8,128)(2,1)S(1)}, u32[]{:S(2)}, u32[]{:S(2)}) collective-permute-start(bf16[160,256]{1,0:T(8,128)(2,1)} %get-tuple-element.10), channel_id=1, source_target_pairs={{0,16},{16,32},{32,0},{1,17},{17,33},{33,1},{2,18},{18,34},{34,2},... | collective-permute-start | bytes 245768 | tf_op jit(solution)/shard_map/ppermute | solution.py:20
  95.9 7.3 %collective-permute-start.4 = (bf16[160,256]{1,0:T(8,128)(2,1)}, bf16[160,256]{1,0:T(8,128)(2,1)S(1)}, u32[]{:S(2)}, u32[]{:S(2)}) collective-permute-start(bf16[160,256]{1,0:T(8,128)(2,1)} %get-tuple-element.11), channel_id=1, source_target_pairs={{0,32},{16,0},{32,16},{1,33},{17,1},{33,17},{2,34},{18,2},{34,18},... | collective-permute-start | bytes 245768 | tf_op jit(solution)/shard_map/ppermute | solution.py:20
  103.2 4.5 %all-to-all-start.2 = ((bf16[16,40,512]{2,1,0:T(8,128)(2,1)}), bf16[16,40,512]{2,1,0:T(8,128)(2,1)}, u32[]{:S(2)}, u32[]{:S(2)}) async-start(bf16[16,40,512]{2,1,0:T(8,128)(2,1)} %get-tuple-element.8), calls=%async_computation.2 | async-start | bytes 1310720 | tf_op jit(solution)/shard_map/all_to_all | solution.py:294
  107.8 13.1 %collective-permute-done.3.refs_4_ = bf16[160,256]{1,0:T(8,128)(2,1)S(1)} collective-permute-done((bf16[160,256]{1,0:T(8,128)(2,1)}, bf16[160,256]{1,0:T(8,128)(2,1)S(1)}, u32[]{:S(2)}, u32[]{:S(2)}) %collective-permute-start.3) | collective-permute-done | bytes 81952 | tf_op jit(solution)/shard_map/ppermute | solution.py:20
  120.9 0.0 collective-permute-done.4.refs_5_
  120.9 0.0 collective-permute-done.2.refs_2_
  120.9 0.0 collective-permute-done.1.refs_1_
  120.9 0.0 copy-start.3
  120.9 0.9 copy-done.3
  121.8 0.0 copy-start
  121.8 3.6 %weight.1 = (bf16[2048,256]{1,0:T(8,128)(2,1)}, f32[8,128]{1,0:T(8,128)S(1)}) custom-call(bf16[16,40,512]{2,1,0:T(8,128)(2,1)} %all-to-all-done.1.rows_ref.refs_0_, bf16[16,40,512]{2,1,0:T(8,128)(2,1)} %collective-permute-done.1.refs_1_, bf16[16,40,512]{2,1,0:T(8,128)(2,1)} %collective-permute-done.2.refs_2_, bf16[160,256]{1,0:T(8,128)(2,1)S(1)} %copy-done.3, ...), custom_call_target="tpu_custom_call" | custom-call | flops 4999999913984 | bytes 4000000 | tf_op jit(solution)/shard_map/weight/pallas_call | solution.py:269
  125.4 6.7 %all-to-all-done.2 = bf16[16,40,512]{2,1,0:T(8,128)(2,1)} async-done(((bf16[16,40,512]{2,1,0:T(8,128)(2,1)}), bf16[16,40,512]{2,1,0:T(8,128)(2,1)}, u32[]{:S(2)}, u32[]{:S(2)}) %all-to-all-start.2) | async-done | bytes 655392 | tf_op jit(solution)/shard_map/all_to_all | solution.py:294
  132.0 0.0 copy-done
  132.0 2.4 %combine.1 = bf16[128,2048]{1,0:T(8,128)(2,1)} custom-call(s32[1,128]{1,0:T(1,128)S(1)} %bitcast.14, bf16[640,512]{1,0:T(8,128)(2,1)} %bitcast.9.rows_hbm, f32[8,128]{1,0:T(8,128)S(1)} %get-tuple-element.12._after_ref), custom_call_target="tpu_custom_call" | custom-call | flops 1000 | bytes 1000 | tf_op jit(solution)/shard_map/combine/pallas_call | solution.py:269
Async XLA Ops:
  0.6 29.0 %copy-start.2 = (f32[1,128,1]{1,2,0:T(1,128)S(1)}, f32[1,128,1]{1,2,0:T(1,128)}, u32[]{:S(2)}) copy-start(f32[1,128,1]{1,2,0:T(1,128)} %param.8) | copy-start | bytes 1540
  3.0 48.3 %copy-start.1 = (bf16[1,1,2048,768]{3,2,1,0:T(8,128)(2,1)S(1)}, bf16[1,1,2048,768]{3,2,1,0:T(8,128)(2,1)}, u32[]{:S(2)}) copy-start(bf16[1,1,2048,768]{3,2,1,0:T(8,128)(2,1)} %param.10) | copy-start | bytes 9437188
  3.0 34.8 %all-to-all-start.1 = ((bf16[16,40,512]{2,1,0:T(8,128)(2,1)}), bf16[16,40,512]{2,1,0:T(8,128)(2,1)}, u32[]{:S(2)}, u32[]{:S(2)}) async-start(bf16[16,40,512]{2,1,0:T(8,128)(2,1)} %bitcast.18), calls=%async_computation.1 | async-start | bytes 1310720 | tf_op jit(solution)/shard_map/all_to_all | solution.py:294
  20.4 9.2 %collective-permute-start = (bf16[1,128,2048]{2,1,0:T(8,128)(2,1)}, bf16[1,128,2048]{2,1,0:T(8,128)(2,1)}, u32[]{:S(2)}, u32[]{:S(2)}) collective-permute-start(bf16[1,128,2048]{2,1,0:T(8,128)(2,1)} %param.9), channel_id=1, source_target_pairs={{0,720},{48,0},{96,48},{144,96},{192,144},{240,192},{288,240},{336... | collective-permute-start | bytes 1572872 | tf_op jit(solution)/shard_map/ppermute | solution.py:20
  37.8 50.0 %all-to-all-start = ((bf16[16,40,512]{2,1,0:T(8,128)(2,1)}), bf16[16,40,512]{2,1,0:T(8,128)(2,1)}, u32[]{:S(2)}, u32[]{:S(2)}) async-start(bf16[16,40,512]{2,1,0:T(8,128)(2,1)} %bitcast.19), calls=%async_computation | async-start | bytes 1310720 | tf_op jit(solution)/shard_map/all_to_all | solution.py:294
  42.1 78.8 %collective-permute-start.2 = (bf16[16,40,512]{2,1,0:T(8,128)(2,1)}, bf16[16,40,512]{2,1,0:T(8,128)(2,1)}, u32[]{:S(2)}, u32[]{:S(2)}) collective-permute-start(bf16[16,40,512]{2,1,0:T(8,128)(2,1)} %all-to-all-done.1.rows_ref.refs_0_), channel_id=1, source_target_pairs={{0,32},{16,0},{32,16},{1,33},{17,1},{33,17},{2,34},{18,2},{34,18},... | collective-permute-start | bytes 1966088 | tf_op jit(solution)/shard_map/ppermute | solution.py:20
  45.4 75.4 %collective-permute-start.1 = (bf16[16,40,512]{2,1,0:T(8,128)(2,1)}, bf16[16,40,512]{2,1,0:T(8,128)(2,1)}, u32[]{:S(2)}, u32[]{:S(2)}) collective-permute-start(bf16[16,40,512]{2,1,0:T(8,128)(2,1)} %all-to-all-done.1.rows_ref.refs_0_), channel_id=1, source_target_pairs={{0,16},{16,32},{32,0},{1,17},{17,33},{33,1},{2,18},{18,34},{34,2},... | collective-permute-start | bytes 1966088 | tf_op jit(solution)/shard_map/ppermute | solution.py:20
  94.0 26.8 %collective-permute-start.3 = (bf16[160,256]{1,0:T(8,128)(2,1)}, bf16[160,256]{1,0:T(8,128)(2,1)S(1)}, u32[]{:S(2)}, u32[]{:S(2)}) collective-permute-start(bf16[160,256]{1,0:T(8,128)(2,1)} %get-tuple-element.10), channel_id=1, source_target_pairs={{0,16},{16,32},{32,0},{1,17},{17,33},{33,1},{2,18},{18,34},{34,2},... | collective-permute-start | bytes 245768 | tf_op jit(solution)/shard_map/ppermute | solution.py:20
  95.9 24.9 %collective-permute-start.4 = (bf16[160,256]{1,0:T(8,128)(2,1)}, bf16[160,256]{1,0:T(8,128)(2,1)S(1)}, u32[]{:S(2)}, u32[]{:S(2)}) collective-permute-start(bf16[160,256]{1,0:T(8,128)(2,1)} %get-tuple-element.11), channel_id=1, source_target_pairs={{0,32},{16,0},{32,16},{1,33},{17,1},{33,17},{2,34},{18,2},{34,18},... | collective-permute-start | bytes 245768 | tf_op jit(solution)/shard_map/ppermute | solution.py:20
  103.2 28.8 %all-to-all-start.2 = ((bf16[16,40,512]{2,1,0:T(8,128)(2,1)}), bf16[16,40,512]{2,1,0:T(8,128)(2,1)}, u32[]{:S(2)}, u32[]{:S(2)}) async-start(bf16[16,40,512]{2,1,0:T(8,128)(2,1)} %get-tuple-element.8), calls=%async_computation.2 | async-start | bytes 1310720 | tf_op jit(solution)/shard_map/all_to_all | solution.py:294
  120.9 0.9 copy-start.3
  121.8 10.3 %copy-start = (s32[1,128,1]{1,2,0:T(1,128)S(1)}, s32[1,128,1]{1,2,0:T(1,128)}, u32[]{:S(2)}) copy-start(s32[1,128,1]{1,2,0:T(1,128)} %param.7) | copy-start | bytes 1540

commit v5 on v4

--- a/solution.py
+++ b/solution.py
@@ -180,6 +180,18 @@
     pre_ref[...] = total
 
 
+def halves_kernel(rows_ref, first_hbm, last_hbm, sems):
+    half = first_hbm.shape[0]
+    copies = [
+        pltpu.make_async_copy(rows_ref.at[i * half : (i + 1) * half], out, sems.at[i])
+        for i, out in enumerate((first_hbm, last_hbm))
+    ]
+    for copy in copies:
+        copy.start()
+    for copy in copies:
+        copy.wait()
+
+
 def expert_kernel(capacity, parts, place_ref, rows_hbm, pre_hbm, w_in_hbm, w_out_hbm,
                   back_ref, own_ref, up_ref, down_ref,
                   hold_ref, held_ref, rows_ref, pre_ref, w_in_ref, w_out_ref, sems, in_sems):
@@ -235,21 +247,24 @@
         copy.wait()
 
 
-def weight_kernel(capacity, *refs):
+def weight_kernel(capacity, own_x_ref, *refs):
     out_ref, done_ref = refs[-2:]
-    refs = refs[:-1]
-    half = (len(refs) - 1) // 2
+    x_refs, grad_refs = refs[:-5], refs[-5:-2]
     done_ref[...] = jnp.zeros(done_ref.shape, F32)
-    chunks, _, short = refs[0].shape
+    chunks, _, short = own_x_ref.shape
     main = capacity // 8 * 8
-    grads = []
-    for ref in refs[half:-1]:
-        grads += [ref[: chunks * main], ref[chunks * main :]]
+    rest = capacity - main
+    grads = [grad_refs[0][...]]
+    for ref in grad_refs[1:]:
+        for i in range(2):
+            at, then = i * chunks * main // 2, chunks * main + i * chunks * rest // 2
+            grads += [ref[at : at + chunks * main // 2], ref[then : then + chunks * rest // 2]]
     grads = jnp.concatenate(grads, axis=0)
-    rests = [packed_rest(capacity, ref) for ref in refs[:half]]
+    x_refs = (own_x_ref, *x_refs)
+    rests = [packed_rest(capacity, ref) for ref in x_refs]
     for p in range(PIECES):
         rows = []
-        for ref, packed in zip(refs[:half], rests, strict=True):
+        for ref, packed in zip(x_refs, rests, strict=True):
             rows += list(whole_piece(capacity, ref, p, packed))
         total = dot(jnp.concatenate(rows, axis=0), grads, ((0,), (0,)))
         out_ref[p * short : (p + 1) * short, :] = total.astype(BF16)
@@ -321,8 +336,12 @@
         flops=10**9,
     )
     recv_g = exchange(send_g.reshape(experts, chunk, short))
-    x_from_below = passed_along(recv_x, "dp", 1)
-    x_from_above = passed_along(recv_x, "dp", -1)
+    lot = pltpu.HBM((experts // 2, chunk, short), BF16)
+    halves = call(
+        halves_kernel, (lot, lot), (recv_x,), out_spec=ANY, scratch=[pltpu.SemaphoreType.DMA((2,))], flops=1000, moved=1000
+    )
+    below = [passed_along(half, "dp", 1) for half in halves]
+    above = [passed_along(half, "dp", -1) for half in halves]
     pre = call(
         functools.partial(pre_kernel, capacity),
         pltpu.HBM((experts * capacity, hidden), F32),
@@ -357,7 +376,7 @@
     grad_in, done = call(
         functools.partial(weight_kernel, capacity),
         (jax.ShapeDtypeStruct((width, hidden // parts), BF16), jax.ShapeDtypeStruct((8, 128), F32)),
-        (recv_x, x_from_below, x_from_above, own, g_from_below, g_from_above),
+        (recv_x, *below, *above, own, g_from_below, g_from_above),
         flops=5*10**12,
     )
     grad_x = call(

time: 135 us -> 133 us (0.985); the launches traced: 134 us -> 131 us
  waiting for transfers between devices: 68.5 us -> 54.1 us
  starting transfers between devices: 44.6 us -> 53.2 us
  local copies, waits for them, and re-layouts: 0.9 us -> 3.58 us
    all_to_all x3, waiting for transfers between devices: 46.2 us -> 35.9 us  [exchange(): lax.all_to_all(rows, AXES, split_axis=0, concat_axis=0, tiled=True, axis_...]
    ppermute x5 -> x7, starting transfers between devices: 18.4 us -> 27.6 us  [passed_along(): return lax.ppermute(value, axis, pairs)]
    ppermute x5 -> x7, waiting for transfers between devices: 22.3 us -> 18.1 us  [passed_along(): return lax.ppermute(value, axis, pairs)]
    unnamed x8 -> x12, local copies, waits for them, and re-layouts: 0.9 us -> 3.58 us
    pallas_call x6 -> x7, Pallas kernels: 19.7 us -> 19.3 us  [call(): pl.pallas_call(kernel, out_shape=outs, in_specs=specs or [VMEM] * len(arg...]
  transfers between devices with their start and end apart: 8 -> 10, of which waited for: 5 -> 6; matrix products, arithmetic and copies ran while one was open for 0% -> 0% of each run, Pallas kernels for 11% -> 11%
where the time goes in v5:
time: 133 us; the launch traced here: 131 us
  waiting for transfers between devices  54.1 us (41%)
  starting transfers between devices  53.2 us (40%)
  Pallas kernels  19.3 us (15%)
  local copies, waits for them, and re-layouts  3.58 us (3%)
    all_to_all x3, waiting for transfers between devices, exchange(): lax.all_to_all(rows, AXES, split_axis=0, concat_axis=0, tiled=True, axis_...  35.9 us
    ppermute x7, starting transfers between devices, passed_along(): return lax.ppermute(value, axis, pairs)  27.6 us
    all_to_all x3, starting transfers between devices, exchange(): lax.all_to_all(rows, AXES, split_axis=0, concat_axis=0, tiled=True, axis_...  25.6 us
    pallas_call x7, Pallas kernels, call(): pl.pallas_call(kernel, out_shape=outs, in_specs=specs or [VMEM] * len(arg...  19.3 us
    ppermute x7, waiting for transfers between devices, passed_along(): return lax.ppermute(value, axis, pairs)  18.1 us
    unnamed x12, local copies, waits for them, and re-layouts  3.58 us
  transfers between devices with their start and end apart: 10, of which 6 were waited for; matrix products, arithmetic and copies ran while one was open for 0% of the time, Pallas kernels for 11%

profile of v5, /device:TPU:1, one launch (start us, length us, event | category | flops | bytes accessed | tf_op | source)
XLA Modules:
  0.0 130.9 jit_solution(7476506122820480392)
XLA Ops:
  0.6 0.0 copy-start.4
  0.6 2.4 %dispatch.3 = bf16[640,512]{1,0:T(8,128)(2,1)} custom-call(s32[1,128]{1,0:T(1,128)} %bitcast.12, bf16[128,2048]{1,0:T(8,128)(2,1)} %bitcast.22), custom_call_target="tpu_custom_call" | custom-call | flops 1000000000 | bytes 4000000 | tf_op jit(solution)/shard_map/dispatch/pallas_call | solution.py:284
  3.1 17.1 %all-to-all-start.1 = ((bf16[16,40,512]{2,1,0:T(8,128)(2,1)}), bf16[16,40,512]{2,1,0:T(8,128)(2,1)S(1)}, u32[]{:S(2)}, u32[]{:S(2)}) async-start(bf16[16,40,512]{2,1,0:T(8,128)(2,1)} %bitcast.19), calls=%async_computation.1 | async-start | bytes 1310720 | tf_op jit(solution)/shard_map/all_to_all | solution.py:309
  20.1 0.0 collective-permute-start
  20.2 8.9 %collective-permute-done = bf16[1,128,2048]{2,1,0:T(8,128)(2,1)S(1)} collective-permute-done((bf16[1,128,2048]{2,1,0:T(8,128)(2,1)S(1)}, bf16[1,128,2048]{2,1,0:T(8,128)(2,1)S(1)}, u32[]{:S(2)}, u32[]{:S(2)}) %collective-permute-start) | collective-permute-done | bytes 524320 | tf_op jit(solution)/shard_map/ppermute | solution.py:20
  29.1 0.8 copy-done.5
  29.9 2.3 %dispatch.2 = bf16[640,512]{1,0:T(8,128)(2,1)} custom-call(f32[1,128]{1,0:T(1,128)S(1)} %bitcast.17, s32[1,128]{1,0:T(1,128)} %bitcast.13, bf16[128,2048]{1,0:T(8,128)(2,1)} %bitcast.23), custom_call_target="tpu_custom_call" | custom-call | flops 1000000000 | bytes 4000000 | tf_op jit(solution)/shard_map/dispatch/pallas_call | solution.py:284
  32.2 5.2 %all-to-all-done.1.rows_ref.own_x_ref = bf16[16,40,512]{2,1,0:T(8,128)(2,1)S(1)} async-done(((bf16[16,40,512]{2,1,0:T(8,128)(2,1)}), bf16[16,40,512]{2,1,0:T(8,128)(2,1)S(1)}, u32[]{:S(2)}, u32[]{:S(2)}) %all-to-all-start.1) | async-done | bytes 655392 | tf_op jit(solution)/shard_map/all_to_all | solution.py:309
  37.5 4.3 %all-to-all-start = ((bf16[16,40,512]{2,1,0:T(8,128)(2,1)}), bf16[16,40,512]{2,1,0:T(8,128)(2,1)}, u32[]{:S(2)}, u32[]{:S(2)}) async-start(bf16[16,40,512]{2,1,0:T(8,128)(2,1)} %bitcast.18), calls=%async_computation | async-start | bytes 1310720 | tf_op jit(solution)/shard_map/all_to_all | solution.py:309
  41.7 0.9 halves.1
  42.6 3.4 %collective-permute-start.3 = (bf16[8,40,512]{2,1,0:T(8,128)(2,1)}, bf16[8,40,512]{2,1,0:T(8,128)(2,1)}, u32[]{:S(2)}, u32[]{:S(2)}) collective-permute-start(bf16[8,40,512]{2,1,0:T(8,128)(2,1)} %get-tuple-element.11), channel_id=1, source_target_pairs={{0,32},{16,0},{32,16},{1,33},{17,1},{33,17},{2,34},{18,2},{34,18},... | collective-permute-start | bytes 983048 | tf_op jit(solution)/shard_map/ppermute | solution.py:20
  46.0 5.8 %collective-permute-start.1 = (bf16[8,40,512]{2,1,0:T(8,128)(2,1)}, bf16[8,40,512]{2,1,0:T(8,128)(2,1)}, u32[]{:S(2)}, u32[]{:S(2)}) collective-permute-start(bf16[8,40,512]{2,1,0:T(8,128)(2,1)} %get-tuple-element.11), channel_id=1, source_target_pairs={{0,16},{16,32},{32,0},{1,17},{17,33},{33,1},{2,18},{18,34},{34,2},... | collective-permute-start | bytes 983048 | tf_op jit(solution)/shard_map/ppermute | solution.py:20
  51.8 3.4 %collective-permute-start.4 = (bf16[8,40,512]{2,1,0:T(8,128)(2,1)}, bf16[8,40,512]{2,1,0:T(8,128)(2,1)}, u32[]{:S(2)}, u32[]{:S(2)}) collective-permute-start(bf16[8,40,512]{2,1,0:T(8,128)(2,1)} %get-tuple-element.12), channel_id=1, source_target_pairs={{0,32},{16,0},{32,16},{1,33},{17,1},{33,17},{2,34},{18,2},{34,18},... | collective-permute-start | bytes 983048 | tf_op jit(solution)/shard_map/ppermute | solution.py:20
  55.2 5.8 %collective-permute-start.2 = (bf16[8,40,512]{2,1,0:T(8,128)(2,1)}, bf16[8,40,512]{2,1,0:T(8,128)(2,1)}, u32[]{:S(2)}, u32[]{:S(2)}) collective-permute-start(bf16[8,40,512]{2,1,0:T(8,128)(2,1)} %get-tuple-element.12), channel_id=1, source_target_pairs={{0,16},{16,32},{32,0},{1,17},{17,33},{33,1},{2,18},{18,34},{34,2},... | collective-permute-start | bytes 983048 | tf_op jit(solution)/shard_map/ppermute | solution.py:20
  61.0 0.0 copy-start.1
  61.0 1.9 %copy-done.1 = bf16[1,1,2048,768]{3,2,1,0:T(8,128)(2,1)S(1)} copy-done((bf16[1,1,2048,768]{3,2,1,0:T(8,128)(2,1)S(1)}, bf16[1,1,2048,768]{3,2,1,0:T(8,128)(2,1)}, u32[]{:S(2)}) %copy-start.1) | copy-done | bytes 3145752
  62.9 1.7 %pre.1.pre_hbm = f32[160,768]{1,0:T(8,128)} custom-call(bf16[16,40,512]{2,1,0:T(8,128)(2,1)S(1)} %all-to-all-done.1.rows_ref.own_x_ref, bf16[2048,768]{1,0:T(8,128)(2,1)S(1)} %bitcast.16), custom_call_target="tpu_custom_call" | custom-call | flops 19999999655936 | bytes 1000 | tf_op jit(solution)/shard_map/pre/pallas_call | solution.py:284
  64.6 29.0 %all-to-all-done.rows_hbm = bf16[16,40,512]{2,1,0:T(8,128)(2,1)} async-done(((bf16[16,40,512]{2,1,0:T(8,128)(2,1)}), bf16[16,40,512]{2,1,0:T(8,128)(2,1)}, u32[]{:S(2)}, u32[]{:S(2)}) %all-to-all-start) | async-done | bytes 655392 | tf_op jit(solution)/shard_map/all_to_all | solution.py:309
  93.6 6.2 %expert.1 = (bf16[16,40,512]{2,1,0:T(8,128)(2,1)}, bf16[160,256]{1,0:T(8,128)(2,1)}, bf16[160,256]{1,0:T(8,128)(2,1)}, bf16[160,256]{1,0:T(8,128)(2,1)}) custom-call(s32[1]{0:T(128)} %bitcast.1.place_ref, bf16[16,40,512]{2,1,0:T(8,128)(2,1)} %all-to-all-done.rows_hbm, f32[160,768]{1,0:T(8,128)} %pre.1.pre_hbm, bf16[2048,768]{1,0:T(8,128)(2,1)} %bitcast.15, ...), custom_call_target="tpu_custom_call" | custom-call | flops 4999999913984 | bytes 1000 | tf_op jit(solution)/shard_map/expert/pallas_call | solution.py:284
  99.9 1.9 %collective-permute-start.5 = (bf16[160,256]{1,0:T(8,128)(2,1)}, bf16[160,256]{1,0:T(8,128)(2,1)S(1)}, u32[]{:S(2)}, u32[]{:S(2)}) collective-permute-start(bf16[160,256]{1,0:T(8,128)(2,1)} %get-tuple-element.14), channel_id=1, source_target_pairs={{0,16},{16,32},{32,0},{1,17},{17,33},{33,1},{2,18},{18,34},{34,2},... | collective-permute-start | bytes 245768 | tf_op jit(solution)/shard_map/ppermute | solution.py:20
  101.8 0.0 collective-permute-done.3.refs_2_
  101.8 7.3 %collective-permute-start.6 = (bf16[160,256]{1,0:T(8,128)(2,1)}, bf16[160,256]{1,0:T(8,128)(2,1)S(1)}, u32[]{:S(2)}, u32[]{:S(2)}) collective-permute-start(bf16[160,256]{1,0:T(8,128)(2,1)} %get-tuple-element.15), channel_id=1, source_target_pairs={{0,32},{16,0},{32,16},{1,33},{17,1},{33,17},{2,34},{18,2},{34,18},... | collective-permute-start | bytes 245768 | tf_op jit(solution)/shard_map/ppermute | solution.py:20
  109.1 4.3 %all-to-all-start.2 = ((bf16[16,40,512]{2,1,0:T(8,128)(2,1)}), bf16[16,40,512]{2,1,0:T(8,128)(2,1)}, u32[]{:S(2)}, u32[]{:S(2)}) async-start(bf16[16,40,512]{2,1,0:T(8,128)(2,1)} %get-tuple-element.10), calls=%async_computation.2 | async-start | bytes 1310720 | tf_op jit(solution)/shard_map/all_to_all | solution.py:309
  113.3 0.0 collective-permute-done.1.refs_0_
  113.4 0.0 collective-permute-done.4.refs_3_
  113.4 0.0 collective-permute-done.2.refs_1_
  113.4 4.8 %collective-permute-done.5.refs_5_ = bf16[160,256]{1,0:T(8,128)(2,1)S(1)} collective-permute-done((bf16[160,256]{1,0:T(8,128)(2,1)}, bf16[160,256]{1,0:T(8,128)(2,1)S(1)}, u32[]{:S(2)}, u32[]{:S(2)}) %collective-permute-start.5) | collective-permute-done | bytes 81952 | tf_op jit(solution)/shard_map/ppermute | solution.py:20
  118.2 4.4 %collective-permute-done.6.refs_6_ = bf16[160,256]{1,0:T(8,128)(2,1)S(1)} collective-permute-done((bf16[160,256]{1,0:T(8,128)(2,1)}, bf16[160,256]{1,0:T(8,128)(2,1)S(1)}, u32[]{:S(2)}, u32[]{:S(2)}) %collective-permute-start.6) | collective-permute-done | bytes 81952 | tf_op jit(solution)/shard_map/ppermute | solution.py:20
  122.6 0.9 copy-done.3
  123.5 3.4 %weight.1 = (bf16[2048,256]{1,0:T(8,128)(2,1)}, f32[8,128]{1,0:T(8,128)S(1)}) custom-call(bf16[16,40,512]{2,1,0:T(8,128)(2,1)S(1)} %all-to-all-done.1.rows_ref.own_x_ref, bf16[8,40,512]{2,1,0:T(8,128)(2,1)} %collective-permute-done.1.refs_0_, bf16[8,40,512]{2,1,0:T(8,128)(2,1)} %collective-permute-done.2.refs_1_, ...), custom_call_target="tpu_custom_call" | custom-call | flops 4999999913984 | bytes 4000000 | tf_op jit(solution)/shard_map/weight/pallas_call | solution.py:284
  126.9 1.7 %all-to-all-done.2 = bf16[16,40,512]{2,1,0:T(8,128)(2,1)} async-done(((bf16[16,40,512]{2,1,0:T(8,128)(2,1)}), bf16[16,40,512]{2,1,0:T(8,128)(2,1)}, u32[]{:S(2)}, u32[]{:S(2)}) %all-to-all-start.2) | async-done | bytes 655392 | tf_op jit(solution)/shard_map/all_to_all | solution.py:309
  128.6 2.4 %combine.1 = bf16[128,2048]{1,0:T(8,128)(2,1)} custom-call(s32[1,128]{1,0:T(1,128)S(1)} %bitcast.14, bf16[640,512]{1,0:T(8,128)(2,1)} %bitcast.9.rows_hbm, f32[8,128]{1,0:T(8,128)S(1)} %get-tuple-element.16._after_ref), custom_call_target="tpu_custom_call" | custom-call | flops 1000 | bytes 1000 | tf_op jit(solution)/shard_map/combine/pallas_call | solution.py:284
  (7 shorter events, 0.0 us)
Async XLA Ops:
  0.6 19.5 %copy-start.4 = (bf16[1,128,2048]{2,1,0:T(8,128)(2,1)S(1)}, bf16[1,128,2048]{2,1,0:T(8,128)(2,1)}, u32[]{:S(2)}) copy-start(bf16[1,128,2048]{2,1,0:T(8,128)(2,1)} %param.9) | copy-start | bytes 1572868
  0.6 29.2 %copy-start.2 = (f32[1,128,1]{1,2,0:T(1,128)S(1)}, f32[1,128,1]{1,2,0:T(1,128)}, u32[]{:S(2)}) copy-start(f32[1,128,1]{1,2,0:T(1,128)} %param.8) | copy-start | bytes 1540
  3.1 34.4 %all-to-all-start.1 = ((bf16[16,40,512]{2,1,0:T(8,128)(2,1)}), bf16[16,40,512]{2,1,0:T(8,128)(2,1)S(1)}, u32[]{:S(2)}, u32[]{:S(2)}) async-start(bf16[16,40,512]{2,1,0:T(8,128)(2,1)} %bitcast.19), calls=%async_computation.1 | async-start | bytes 1310720 | tf_op jit(solution)/shard_map/all_to_all | solution.py:309
  20.1 8.9 %collective-permute-start = (bf16[1,128,2048]{2,1,0:T(8,128)(2,1)S(1)}, bf16[1,128,2048]{2,1,0:T(8,128)(2,1)S(1)}, u32[]{:S(2)}, u32[]{:S(2)}) collective-permute-start(bf16[1,128,2048]{2,1,0:T(8,128)(2,1)S(1)} %copy-done.4), channel_id=1, source_target_pairs={{0,720},{48,0},{96,48},{144,96},{192,144},{240,192},{288,240},{336... | collective-permute-start | bytes 1572872 | tf_op jit(solution)/shard_map/ppermute | solution.py:20
  29.1 0.8 copy-start.5
  37.5 56.2 %all-to-all-start = ((bf16[16,40,512]{2,1,0:T(8,128)(2,1)}), bf16[16,40,512]{2,1,0:T(8,128)(2,1)}, u32[]{:S(2)}, u32[]{:S(2)}) async-start(bf16[16,40,512]{2,1,0:T(8,128)(2,1)} %bitcast.18), calls=%async_computation | async-start | bytes 1310720 | tf_op jit(solution)/shard_map/all_to_all | solution.py:309
  42.6 59.2 %collective-permute-start.3 = (bf16[8,40,512]{2,1,0:T(8,128)(2,1)}, bf16[8,40,512]{2,1,0:T(8,128)(2,1)}, u32[]{:S(2)}, u32[]{:S(2)}) collective-permute-start(bf16[8,40,512]{2,1,0:T(8,128)(2,1)} %get-tuple-element.11), channel_id=1, source_target_pairs={{0,32},{16,0},{32,16},{1,33},{17,1},{33,17},{2,34},{18,2},{34,18},... | collective-permute-start | bytes 983048 | tf_op jit(solution)/shard_map/ppermute | solution.py:20
  46.0 67.4 %collective-permute-start.1 = (bf16[8,40,512]{2,1,0:T(8,128)(2,1)}, bf16[8,40,512]{2,1,0:T(8,128)(2,1)}, u32[]{:S(2)}, u32[]{:S(2)}) collective-permute-start(bf16[8,40,512]{2,1,0:T(8,128)(2,1)} %get-tuple-element.11), channel_id=1, source_target_pairs={{0,16},{16,32},{32,0},{1,17},{17,33},{33,1},{2,18},{18,34},{34,2},... | collective-permute-start | bytes 983048 | tf_op jit(solution)/shard_map/ppermute | solution.py:20
  51.8 61.6 %collective-permute-start.4 = (bf16[8,40,512]{2,1,0:T(8,128)(2,1)}, bf16[8,40,512]{2,1,0:T(8,128)(2,1)}, u32[]{:S(2)}, u32[]{:S(2)}) collective-permute-start(bf16[8,40,512]{2,1,0:T(8,128)(2,1)} %get-tuple-element.12), channel_id=1, source_target_pairs={{0,32},{16,0},{32,16},{1,33},{17,1},{33,17},{2,34},{18,2},{34,18},... | collective-permute-start | bytes 983048 | tf_op jit(solution)/shard_map/ppermute | solution.py:20
  55.2 58.2 %collective-permute-start.2 = (bf16[8,40,512]{2,1,0:T(8,128)(2,1)}, bf16[8,40,512]{2,1,0:T(8,128)(2,1)}, u32[]{:S(2)}, u32[]{:S(2)}) collective-permute-start(bf16[8,40,512]{2,1,0:T(8,128)(2,1)} %get-tuple-element.12), channel_id=1, source_target_pairs={{0,16},{16,32},{32,0},{1,17},{17,33},{33,1},{2,18},{18,34},{34,2},... | collective-permute-start | bytes 983048 | tf_op jit(solution)/shard_map/ppermute | solution.py:20
  61.0 1.9 %copy-start.1 = (bf16[1,1,2048,768]{3,2,1,0:T(8,128)(2,1)S(1)}, bf16[1,1,2048,768]{3,2,1,0:T(8,128)(2,1)}, u32[]{:S(2)}) copy-start(bf16[1,1,2048,768]{3,2,1,0:T(8,128)(2,1)} %param.10) | copy-start | bytes 9437188
  99.9 18.4 %collective-permute-start.5 = (bf16[160,256]{1,0:T(8,128)(2,1)}, bf16[160,256]{1,0:T(8,128)(2,1)S(1)}, u32[]{:S(2)}, u32[]{:S(2)}) collective-permute-start(bf16[160,256]{1,0:T(8,128)(2,1)} %get-tuple-element.14), channel_id=1, source_target_pairs={{0,16},{16,32},{32,0},{1,17},{17,33},{33,1},{2,18},{18,34},{34,2},... | collective-permute-start | bytes 245768 | tf_op jit(solution)/shard_map/ppermute | solution.py:20
  101.8 20.8 %collective-permute-start.6 = (bf16[160,256]{1,0:T(8,128)(2,1)}, bf16[160,256]{1,0:T(8,128)(2,1)S(1)}, u32[]{:S(2)}, u32[]{:S(2)}) collective-permute-start(bf16[160,256]{1,0:T(8,128)(2,1)} %get-tuple-element.15), channel_id=1, source_target_pairs={{0,32},{16,0},{32,16},{1,33},{17,1},{33,17},{2,34},{18,2},{34,18},... | collective-permute-start | bytes 245768 | tf_op jit(solution)/shard_map/ppermute | solution.py:20
  109.1 19.5 %all-to-all-start.2 = ((bf16[16,40,512]{2,1,0:T(8,128)(2,1)}), bf16[16,40,512]{2,1,0:T(8,128)(2,1)}, u32[]{:S(2)}, u32[]{:S(2)}) async-start(bf16[16,40,512]{2,1,0:T(8,128)(2,1)} %get-tuple-element.10), calls=%async_computation.2 | async-start | bytes 1310720 | tf_op jit(solution)/shard_map/all_to_all | solution.py:309
  122.6 0.9 copy-start.3
  123.5 5.1 %copy-start = (s32[1,128,1]{1,2,0:T(1,128)S(1)}, s32[1,128,1]{1,2,0:T(1,128)}, u32[]{:S(2)}) copy-start(s32[1,128,1]{1,2,0:T(1,128)} %param.7) | copy-start | bytes 1540

commit v6 on v5

--- a/solution.py
+++ b/solution.py
@@ -333,7 +333,7 @@
         specs=[VMEM, ANY, ANY],
         out_spec=ANY,
         scratch=scratch,
-        flops=10**9,
+        flops=2*10**13,
     )
     recv_g = exchange(send_g.reshape(experts, chunk, short))
     lot = pltpu.HBM((experts // 2, chunk, short), BF16)

time: 133 us -> 134 us (level)
  starting transfers between devices: 53.2 us -> 57.7 us
  waiting for transfers between devices: 54.1 us -> 49.7 us
  Pallas kernels: 19.3 us -> 21.7 us
  local copies, waits for them, and re-layouts: 3.58 us -> 1.69 us
    ppermute x7, starting transfers between devices: 27.6 us -> 38.1 us  [passed_along(): return lax.ppermute(value, axis, pairs)]
    ppermute x7, waiting for transfers between devices: 18.1 us -> 8.18 us  [passed_along(): return lax.ppermute(value, axis, pairs)]
    all_to_all x3, starting transfers between devices: 25.6 us -> 19.6 us  [exchange(): lax.all_to_all(rows, AXES, split_axis=0, concat_axis=0, tiled=True, axis_...]
    all_to_all x3, waiting for transfers between devices: 35.9 us -> 41.5 us  [exchange(): lax.all_to_all(rows, AXES, split_axis=0, concat_axis=0, tiled=True, axis_...]
    pallas_call x7, Pallas kernels: 19.3 us -> 21.7 us  [call(): pl.pallas_call(kernel, out_shape=outs, in_specs=specs or [VMEM] * len(arg...]
    unnamed x12 -> x10, local copies, waits for them, and re-layouts: 3.58 us -> 1.69 us
  transfers between devices with their start and end apart: 10 -> 10, of which waited for: 6 -> 4; matrix products, arithmetic and copies ran while one was open for 0% -> 0% of each run, Pallas kernels for 11% -> 15%
where the time goes in v6:
time: 134 us; the launch traced here: 132 us
  starting transfers between devices  57.7 us (43%)
  waiting for transfers between devices  49.7 us (37%)
  Pallas kernels  21.7 us (16%)
  local copies, waits for them, and re-layouts  1.69 us (1%)
    all_to_all x3, waiting for transfers between devices, exchange(): lax.all_to_all(rows, AXES, split_axis=0, concat_axis=0, tiled=True, axis_...  41.5 us
    ppermute x7, starting transfers between devices, passed_along(): return lax.ppermute(value, axis, pairs)  38.1 us
    pallas_call x7, Pallas kernels, call(): pl.pallas_call(kernel, out_shape=outs, in_specs=specs or [VMEM] * len(arg...  21.7 us
    all_to_all x3, starting transfers between devices, exchange(): lax.all_to_all(rows, AXES, split_axis=0, concat_axis=0, tiled=True, axis_...  19.6 us
    ppermute x7, waiting for transfers between devices, passed_along(): return lax.ppermute(value, axis, pairs)  8.18 us
  transfers between devices with their start and end apart: 10, of which 4 were waited for; matrix products, arithmetic and copies ran while one was open for 0% of the time, Pallas kernels for 15%

profile of v6, /device:TPU:1, one launch (start us, length us, event | category | flops | bytes accessed | tf_op | source)
XLA Modules:
  0.0 131.7 jit_solution(2735473995188419471)
XLA Ops:
  0.6 10.5 %collective-permute-start = (bf16[1,128,2048]{2,1,0:T(8,128)(2,1)}, bf16[1,128,2048]{2,1,0:T(8,128)(2,1)S(1)}, u32[]{:S(2)}, u32[]{:S(2)}) collective-permute-start(bf16[1,128,2048]{2,1,0:T(8,128)(2,1)} %param.9), channel_id=1, source_target_pairs={{0,720},{48,0},{96,48},{144,96},{192,144},{240,192},{288,240},{336... | collective-permute-start | bytes 1572872 | tf_op jit(solution)/shard_map/ppermute | solution.py:20
  11.2 2.4 %dispatch.3 = bf16[640,512]{1,0:T(8,128)(2,1)} custom-call(s32[1,128]{1,0:T(1,128)} %bitcast.12, bf16[128,2048]{1,0:T(8,128)(2,1)} %bitcast.22), custom_call_target="tpu_custom_call" | custom-call | flops 1000000000 | bytes 4000000 | tf_op jit(solution)/shard_map/dispatch/pallas_call | solution.py:284
  13.5 7.3 %all-to-all-start.1 = ((bf16[16,40,512]{2,1,0:T(8,128)(2,1)}), bf16[16,40,512]{2,1,0:T(8,128)(2,1)}, u32[]{:S(2)}, u32[]{:S(2)}) async-start(bf16[16,40,512]{2,1,0:T(8,128)(2,1)} %bitcast.19), calls=%async_computation.1 | async-start | bytes 1310720 | tf_op jit(solution)/shard_map/all_to_all | solution.py:309
  20.8 0.0 collective-permute-done
  20.8 0.0 copy-start.4
  20.9 0.8 copy-done.4
  21.6 0.0 copy-done.2
  21.6 2.5 %dispatch.2 = bf16[640,512]{1,0:T(8,128)(2,1)} custom-call(f32[1,128]{1,0:T(1,128)S(1)} %bitcast.17, s32[1,128]{1,0:T(1,128)} %bitcast.13, bf16[128,2048]{1,0:T(8,128)(2,1)} %bitcast.23), custom_call_target="tpu_custom_call" | custom-call | flops 19999999655936 | bytes 4000000 | tf_op jit(solution)/shard_map/dispatch/pallas_call | solution.py:284
  24.1 14.1 %all-to-all-done.1.rows_ref.own_x_ref = bf16[16,40,512]{2,1,0:T(8,128)(2,1)} async-done(((bf16[16,40,512]{2,1,0:T(8,128)(2,1)}), bf16[16,40,512]{2,1,0:T(8,128)(2,1)}, u32[]{:S(2)}, u32[]{:S(2)}) %all-to-all-start.1) | async-done | bytes 655392 | tf_op jit(solution)/shard_map/all_to_all | solution.py:309
  38.2 4.3 %all-to-all-start = ((bf16[16,40,512]{2,1,0:T(8,128)(2,1)}), bf16[16,40,512]{2,1,0:T(8,128)(2,1)}, u32[]{:S(2)}, u32[]{:S(2)}) async-start(bf16[16,40,512]{2,1,0:T(8,128)(2,1)} %bitcast.18), calls=%async_computation | async-start | bytes 1310720 | tf_op jit(solution)/shard_map/all_to_all | solution.py:309
  42.5 1.9 %halves.1 = (bf16[8,40,512]{2,1,0:T(8,128)(2,1)}, bf16[8,40,512]{2,1,0:T(8,128)(2,1)}) custom-call(bf16[16,40,512]{2,1,0:T(8,128)(2,1)} %all-to-all-done.1.rows_ref.own_x_ref), custom_call_target="tpu_custom_call" | custom-call | flops 1000 | bytes 1000 | tf_op jit(solution)/shard_map/halves/pallas_call | solution.py:284
  44.4 3.4 %collective-permute-start.3 = (bf16[8,40,512]{2,1,0:T(8,128)(2,1)}, bf16[8,40,512]{2,1,0:T(8,128)(2,1)}, u32[]{:S(2)}, u32[]{:S(2)}) collective-permute-start(bf16[8,40,512]{2,1,0:T(8,128)(2,1)} %get-tuple-element.11), channel_id=1, source_target_pairs={{0,32},{16,0},{32,16},{1,33},{17,1},{33,17},{2,34},{18,2},{34,18},... | collective-permute-start | bytes 983048 | tf_op jit(solution)/shard_map/ppermute | solution.py:20
  47.8 5.8 %collective-permute-start.1 = (bf16[8,40,512]{2,1,0:T(8,128)(2,1)}, bf16[8,40,512]{2,1,0:T(8,128)(2,1)}, u32[]{:S(2)}, u32[]{:S(2)}) collective-permute-start(bf16[8,40,512]{2,1,0:T(8,128)(2,1)} %get-tuple-element.11), channel_id=1, source_target_pairs={{0,16},{16,32},{32,0},{1,17},{17,33},{33,1},{2,18},{18,34},{34,2},... | collective-permute-start | bytes 983048 | tf_op jit(solution)/shard_map/ppermute | solution.py:20
  53.6 3.4 %collective-permute-start.4 = (bf16[8,40,512]{2,1,0:T(8,128)(2,1)}, bf16[8,40,512]{2,1,0:T(8,128)(2,1)}, u32[]{:S(2)}, u32[]{:S(2)}) collective-permute-start(bf16[8,40,512]{2,1,0:T(8,128)(2,1)} %get-tuple-element.12), channel_id=1, source_target_pairs={{0,32},{16,0},{32,16},{1,33},{17,1},{33,17},{2,34},{18,2},{34,18},... | collective-permute-start | bytes 983048 | tf_op jit(solution)/shard_map/ppermute | solution.py:20
  57.0 5.8 %collective-permute-start.2 = (bf16[8,40,512]{2,1,0:T(8,128)(2,1)}, bf16[8,40,512]{2,1,0:T(8,128)(2,1)}, u32[]{:S(2)}, u32[]{:S(2)}) collective-permute-start(bf16[8,40,512]{2,1,0:T(8,128)(2,1)} %get-tuple-element.12), channel_id=1, source_target_pairs={{0,16},{16,32},{32,0},{1,17},{17,33},{33,1},{2,18},{18,34},{34,2},... | collective-permute-start | bytes 983048 | tf_op jit(solution)/shard_map/ppermute | solution.py:20
  62.8 2.8 %pre.1.pre_hbm = f32[160,768]{1,0:T(8,128)} custom-call(bf16[16,40,512]{2,1,0:T(8,128)(2,1)} %all-to-all-done.1.rows_ref.own_x_ref, bf16[2048,768]{1,0:T(8,128)(2,1)S(1)} %bitcast.16), custom_call_target="tpu_custom_call" | custom-call | flops 19999999655936 | bytes 1000 | tf_op jit(solution)/shard_map/pre/pallas_call | solution.py:284
  65.7 24.3 %all-to-all-done.rows_hbm = bf16[16,40,512]{2,1,0:T(8,128)(2,1)} async-done(((bf16[16,40,512]{2,1,0:T(8,128)(2,1)}), bf16[16,40,512]{2,1,0:T(8,128)(2,1)}, u32[]{:S(2)}, u32[]{:S(2)}) %all-to-all-start) | async-done | bytes 655392 | tf_op jit(solution)/shard_map/all_to_all | solution.py:309
  90.0 6.2 %expert.1 = (bf16[16,40,512]{2,1,0:T(8,128)(2,1)}, bf16[160,256]{1,0:T(8,128)(2,1)}, bf16[160,256]{1,0:T(8,128)(2,1)}, bf16[160,256]{1,0:T(8,128)(2,1)}) custom-call(s32[1]{0:T(128)} %bitcast.1.place_ref, bf16[16,40,512]{2,1,0:T(8,128)(2,1)} %all-to-all-done.rows_hbm, f32[160,768]{1,0:T(8,128)} %pre.1.pre_hbm, bf16[2048,768]{1,0:T(8,128)(2,1)} %bitcast.15, ...), custom_call_target="tpu_custom_call" | custom-call | flops 4999999913984 | bytes 1000 | tf_op jit(solution)/shard_map/expert/pallas_call | solution.py:284
  96.2 1.9 %collective-permute-start.5 = (bf16[160,256]{1,0:T(8,128)(2,1)}, bf16[160,256]{1,0:T(8,128)(2,1)S(1)}, u32[]{:S(2)}, u32[]{:S(2)}) collective-permute-start(bf16[160,256]{1,0:T(8,128)(2,1)} %get-tuple-element.14), channel_id=1, source_target_pairs={{0,16},{16,32},{32,0},{1,17},{17,33},{33,1},{2,18},{18,34},{34,2},... | collective-permute-start | bytes 245768 | tf_op jit(solution)/shard_map/ppermute | solution.py:20
  98.1 0.0 collective-permute-done.3.refs_2_
  98.1 7.3 %collective-permute-start.6 = (bf16[160,256]{1,0:T(8,128)(2,1)}, bf16[160,256]{1,0:T(8,128)(2,1)S(1)}, u32[]{:S(2)}, u32[]{:S(2)}) collective-permute-start(bf16[160,256]{1,0:T(8,128)(2,1)} %get-tuple-element.15), channel_id=1, source_target_pairs={{0,32},{16,0},{32,16},{1,33},{17,1},{33,17},{2,34},{18,2},{34,18},... | collective-permute-start | bytes 245768 | tf_op jit(solution)/shard_map/ppermute | solution.py:20
  105.4 8.1 %all-to-all-start.2 = ((bf16[16,40,512]{2,1,0:T(8,128)(2,1)}), bf16[16,40,512]{2,1,0:T(8,128)(2,1)}, u32[]{:S(2)}, u32[]{:S(2)}) async-start(bf16[16,40,512]{2,1,0:T(8,128)(2,1)} %get-tuple-element.10), calls=%async_computation.2 | async-start | bytes 1310720 | tf_op jit(solution)/shard_map/all_to_all | solution.py:309
  113.5 0.0 collective-permute-done.1.refs_0_
  113.5 0.0 collective-permute-done.4.refs_3_
  113.5 0.0 collective-permute-done.2.refs_1_
  113.5 8.2 %collective-permute-done.5.refs_5_ = bf16[160,256]{1,0:T(8,128)(2,1)S(1)} collective-permute-done((bf16[160,256]{1,0:T(8,128)(2,1)}, bf16[160,256]{1,0:T(8,128)(2,1)S(1)}, u32[]{:S(2)}, u32[]{:S(2)}) %collective-permute-start.5) | collective-permute-done | bytes 81952 | tf_op jit(solution)/shard_map/ppermute | solution.py:20
  121.7 0.0 collective-permute-done.6.refs_6_
  121.7 0.9 copy-done.3
  122.6 3.6 %weight.1 = (bf16[2048,256]{1,0:T(8,128)(2,1)}, f32[8,128]{1,0:T(8,128)S(1)}) custom-call(bf16[16,40,512]{2,1,0:T(8,128)(2,1)} %all-to-all-done.1.rows_ref.own_x_ref, bf16[8,40,512]{2,1,0:T(8,128)(2,1)} %collective-permute-done.1.refs_0_, bf16[8,40,512]{2,1,0:T(8,128)(2,1)} %collective-permute-done.2.refs_1_, ...), custom_call_target="tpu_custom_call" | custom-call | flops 4999999913984 | bytes 4000000 | tf_op jit(solution)/shard_map/weight/pallas_call | solution.py:284
  126.2 3.1 %all-to-all-done.2 = bf16[16,40,512]{2,1,0:T(8,128)(2,1)} async-done(((bf16[16,40,512]{2,1,0:T(8,128)(2,1)}), bf16[16,40,512]{2,1,0:T(8,128)(2,1)}, u32[]{:S(2)}, u32[]{:S(2)}) %all-to-all-start.2) | async-done | bytes 655392 | tf_op jit(solution)/shard_map/all_to_all | solution.py:309
  129.3 0.0 copy-done
  129.3 2.4 %combine.1 = bf16[128,2048]{1,0:T(8,128)(2,1)} custom-call(s32[1,128]{1,0:T(1,128)S(1)} %bitcast.14, bf16[640,512]{1,0:T(8,128)(2,1)} %bitcast.9.rows_hbm, f32[8,128]{1,0:T(8,128)S(1)} %get-tuple-element.16._after_ref), custom_call_target="tpu_custom_call" | custom-call | flops 1000 | bytes 1000 | tf_op jit(solution)/shard_map/combine/pallas_call | solution.py:284
  (5 shorter events, 0.0 us)
Async XLA Ops:
  0.6 21.0 %copy-start.2 = (f32[1,128,1]{1,2,0:T(1,128)S(1)}, f32[1,128,1]{1,2,0:T(1,128)}, u32[]{:S(2)}) copy-start(f32[1,128,1]{1,2,0:T(1,128)} %param.8) | copy-start | bytes 1540
  0.6 20.2 %collective-permute-start = (bf16[1,128,2048]{2,1,0:T(8,128)(2,1)}, bf16[1,128,2048]{2,1,0:T(8,128)(2,1)S(1)}, u32[]{:S(2)}, u32[]{:S(2)}) collective-permute-start(bf16[1,128,2048]{2,1,0:T(8,128)(2,1)} %param.9), channel_id=1, source_target_pairs={{0,720},{48,0},{96,48},{144,96},{192,144},{240,192},{288,240},{336... | collective-permute-start | bytes 1572872 | tf_op jit(solution)/shard_map/ppermute | solution.py:20
  13.5 24.7 %all-to-all-start.1 = ((bf16[16,40,512]{2,1,0:T(8,128)(2,1)}), bf16[16,40,512]{2,1,0:T(8,128)(2,1)}, u32[]{:S(2)}, u32[]{:S(2)}) async-start(bf16[16,40,512]{2,1,0:T(8,128)(2,1)} %bitcast.19), calls=%async_computation.1 | async-start | bytes 1310720 | tf_op jit(solution)/shard_map/all_to_all | solution.py:309
  20.8 0.8 copy-start.4
  21.6 41.2 %copy-start.1 = (bf16[1,1,2048,768]{3,2,1,0:T(8,128)(2,1)S(1)}, bf16[1,1,2048,768]{3,2,1,0:T(8,128)(2,1)}, u32[]{:S(2)}) copy-start(bf16[1,1,2048,768]{3,2,1,0:T(8,128)(2,1)} %param.10) | copy-start | bytes 9437188
  38.2 51.8 %all-to-all-start = ((bf16[16,40,512]{2,1,0:T(8,128)(2,1)}), bf16[16,40,512]{2,1,0:T(8,128)(2,1)}, u32[]{:S(2)}, u32[]{:S(2)}) async-start(bf16[16,40,512]{2,1,0:T(8,128)(2,1)} %bitcast.18), calls=%async_computation | async-start | bytes 1310720 | tf_op jit(solution)/shard_map/all_to_all | solution.py:309
  44.4 53.7 %collective-permute-start.3 = (bf16[8,40,512]{2,1,0:T(8,128)(2,1)}, bf16[8,40,512]{2,1,0:T(8,128)(2,1)}, u32[]{:S(2)}, u32[]{:S(2)}) collective-permute-start(bf16[8,40,512]{2,1,0:T(8,128)(2,1)} %get-tuple-element.11), channel_id=1, source_target_pairs={{0,32},{16,0},{32,16},{1,33},{17,1},{33,17},{2,34},{18,2},{34,18},... | collective-permute-start | bytes 983048 | tf_op jit(solution)/shard_map/ppermute | solution.py:20
  47.8 65.7 %collective-permute-start.1 = (bf16[8,40,512]{2,1,0:T(8,128)(2,1)}, bf16[8,40,512]{2,1,0:T(8,128)(2,1)}, u32[]{:S(2)}, u32[]{:S(2)}) collective-permute-start(bf16[8,40,512]{2,1,0:T(8,128)(2,1)} %get-tuple-element.11), channel_id=1, source_target_pairs={{0,16},{16,32},{32,0},{1,17},{17,33},{33,1},{2,18},{18,34},{34,2},... | collective-permute-start | bytes 983048 | tf_op jit(solution)/shard_map/ppermute | solution.py:20
  53.6 59.9 %collective-permute-start.4 = (bf16[8,40,512]{2,1,0:T(8,128)(2,1)}, bf16[8,40,512]{2,1,0:T(8,128)(2,1)}, u32[]{:S(2)}, u32[]{:S(2)}) collective-permute-start(bf16[8,40,512]{2,1,0:T(8,128)(2,1)} %get-tuple-element.12), channel_id=1, source_target_pairs={{0,32},{16,0},{32,16},{1,33},{17,1},{33,17},{2,34},{18,2},{34,18},... | collective-permute-start | bytes 983048 | tf_op jit(solution)/shard_map/ppermute | solution.py:20
  57.0 56.5 %collective-permute-start.2 = (bf16[8,40,512]{2,1,0:T(8,128)(2,1)}, bf16[8,40,512]{2,1,0:T(8,128)(2,1)}, u32[]{:S(2)}, u32[]{:S(2)}) collective-permute-start(bf16[8,40,512]{2,1,0:T(8,128)(2,1)} %get-tuple-element.12), channel_id=1, source_target_pairs={{0,16},{16,32},{32,0},{1,17},{17,33},{33,1},{2,18},{18,34},{34,2},... | collective-permute-start | bytes 983048 | tf_op jit(solution)/shard_map/ppermute | solution.py:20
  96.2 25.5 %collective-permute-start.5 = (bf16[160,256]{1,0:T(8,128)(2,1)}, bf16[160,256]{1,0:T(8,128)(2,1)S(1)}, u32[]{:S(2)}, u32[]{:S(2)}) collective-permute-start(bf16[160,256]{1,0:T(8,128)(2,1)} %get-tuple-element.14), channel_id=1, source_target_pairs={{0,16},{16,32},{32,0},{1,17},{17,33},{33,1},{2,18},{18,34},{34,2},... | collective-permute-start | bytes 245768 | tf_op jit(solution)/shard_map/ppermute | solution.py:20
  98.1 23.5 %collective-permute-start.6 = (bf16[160,256]{1,0:T(8,128)(2,1)}, bf16[160,256]{1,0:T(8,128)(2,1)S(1)}, u32[]{:S(2)}, u32[]{:S(2)}) collective-permute-start(bf16[160,256]{1,0:T(8,128)(2,1)} %get-tuple-element.15), channel_id=1, source_target_pairs={{0,32},{16,0},{32,16},{1,33},{17,1},{33,17},{2,34},{18,2},{34,18},... | collective-permute-start | bytes 245768 | tf_op jit(solution)/shard_map/ppermute | solution.py:20
  105.4 23.9 %all-to-all-start.2 = ((bf16[16,40,512]{2,1,0:T(8,128)(2,1)}), bf16[16,40,512]{2,1,0:T(8,128)(2,1)}, u32[]{:S(2)}, u32[]{:S(2)}) async-start(bf16[16,40,512]{2,1,0:T(8,128)(2,1)} %get-tuple-element.10), calls=%async_computation.2 | async-start | bytes 1310720 | tf_op jit(solution)/shard_map/all_to_all | solution.py:309
  121.7 0.9 copy-start.3
  122.6 6.7 %copy-start = (s32[1,128,1]{1,2,0:T(1,128)S(1)}, s32[1,128,1]{1,2,0:T(1,128)}, u32[]{:S(2)}) copy-start(s32[1,128,1]{1,2,0:T(1,128)} %param.7) | copy-start | bytes 1540
